TPU v7x, 1024 devices: a whole 4x4x32 slice. The times are simulated.
1024 devices in a mesh: pipe: 64 (over y_lo, z), tensor: 16 (over x, y_hi, core).
Axes of the slice: x: 4, y: 4 (y_hi: 2, y_lo: 2; y = y_hi * 2 + y_lo), z: 32, core: 2. Of those that a mesh axis runs over, the one named last changes fastest.
Arguments:
- residual: bfloat16 [64, 128, 4096], P('pipe'), may hold values from -4 to 4
- out_proj: bfloat16 [64, 4096, 4096], P('pipe', 'tensor'), may hold values from -0.25 to 0.25
- attn_in: bfloat16 [64, 3, 128, 4096], P('pipe', None, None, 'tensor'), may hold values from -9 to 9
- stash_slots: bfloat16 [64, 2, 3, 128, 4096], P('pipe', None, None, None, 'tensor'), may hold values from -9 to 9
- grad_in: bfloat16 [64, 128, 4096], P('pipe'), may hold values from -6 to 6
- stash_slot: int32 [64], replicated, may hold values from 0 to 1
Outputs:
- fwd_out: bfloat16 [64, 128, 4096], P('pipe')
- qkv_grad: bfloat16 [64, 3, 128, 4096], P('pipe', None, None, 'tensor')
- evicted: bfloat16 [64, 3, 128, 4096], P('pipe', None, None, 'tensor')
All inputs are finite; a program needn't handle non-finite values.
Results may differ from a plain program's by a relative error of at most 0.0065.
Values may be sent and summed in bfloat16 or wider, within the bound.
No kernel may reach another device: no remote copies, remote signals or barrier semaphores. Data moves between devices by JAX's collectives and lax.ppermute only.
A program may use at most 32 MiB of HBM per device.

v0:
```python
import jax
import jax.numpy as jnp
from jax import lax
from jax.sharding import PartitionSpec as P

HD = 128


def cut_along(value, dim, count):
    before, after = (value.shape[:dim], value.shape[dim + 1 :])
    return jnp.moveaxis(value.reshape(*before, count, -1, *after), dim, 0)


def summed_on_arrival(value, axis, dim):
    count = lax.axis_size(axis)
    blocks = lax.all_to_all(cut_along(value, dim, count), axis, 0, 0, tiled=True)
    return jnp.sum(blocks, axis=0)


def shifted(block, axis, distance):
    devices = range(lax.axis_size(axis))
    route = [((i - distance) % len(devices), i) for i in devices]
    return lax.ppermute(block, axis, route)


def in_order(blocks, dim):
    blocks = jnp.moveaxis(blocks, 0, dim)
    shape = blocks.shape
    return blocks.reshape(*shape[:dim], shape[dim] * shape[dim + 1], *shape[dim + 2 :])


def sent_to_all(value, axis):
    count = lax.axis_size(axis)
    return lax.all_to_all(
        jnp.broadcast_to(value[None], (count, *value.shape)), axis, 0, 0, tiled=True
    )


def gathered_copies(value, axis, dim):
    return in_order(sent_to_all(value, axis), dim)


def head_probs(query_in, key_in):
    length = query_in.shape[0]
    query_heads = query_in.astype(jnp.float32).reshape(length, -1, HD)
    key_heads = key_in.astype(jnp.float32).reshape(length, -1, HD)
    scores = jnp.einsum("ihd,jhd->hij", query_heads, key_heads) * HD ** (-0.5)
    row_ids = jnp.arange(length, dtype=jnp.int32)
    allowed = row_ids[:, None] >= row_ids[None, :]
    scores = jnp.where(allowed[None], scores, -jnp.inf)
    return jax.nn.softmax(scores, axis=-1)


def attend(inputs):
    length = inputs.shape[1]
    attn_probs = head_probs(inputs[0], inputs[1])
    probs_low = lax.optimization_barrier(attn_probs.astype(jnp.bfloat16)).astype(jnp.float32)
    value_heads = inputs[2].astype(jnp.float32).reshape(length, -1, HD)
    context = jnp.einsum("hij,jhd->ihd", probs_low, value_heads)
    return context.reshape(length, -1).astype(jnp.bfloat16)


def attend_back(stored, grad_context):
    length = stored.shape[1]
    scale_factor = HD ** (-0.5)
    attn_probs = head_probs(stored[0], stored[1])
    grad_heads = lax.optimization_barrier(grad_context).astype(jnp.float32).reshape(length, -1, HD)
    query_heads = stored[0].astype(jnp.float32).reshape(length, -1, HD)
    key_heads = stored[1].astype(jnp.float32).reshape(length, -1, HD)
    value_heads = stored[2].astype(jnp.float32).reshape(length, -1, HD)
    grad_probs = jnp.einsum("ihd,jhd->hij", grad_heads, value_heads)
    row_delta = jnp.sum(attn_probs * grad_probs, axis=-1, keepdims=True)
    grad_scores = (attn_probs * (grad_probs - row_delta)).astype(jnp.bfloat16)
    grad_scores = lax.optimization_barrier(grad_scores).astype(jnp.float32)
    probs_low = lax.optimization_barrier(attn_probs.astype(jnp.bfloat16)).astype(jnp.float32)
    grad_query = jnp.einsum("hij,jhd->ihd", grad_scores, key_heads) * scale_factor
    grad_key = jnp.einsum("hij,ihd->jhd", grad_scores, query_heads) * scale_factor
    grad_value = jnp.einsum("hij,ihd->jhd", probs_low, grad_heads)
    stacked = jnp.stack([grad_query, grad_key, grad_value], axis=0)
    return stacked.reshape(3, length, -1).astype(jnp.bfloat16)


def on_device(residual, out_proj, attn_in, stash_slots, grad_in, stash_slot):
    sections = lax.axis_size("pipe")
    half_way = sections // 2
    own_section = lax.axis_index("pipe")
    partner = (own_section + half_way) % sections
    wanted_slot = lax.dynamic_index_in_dim(stash_slot, partner, 0, keepdims=False)
    request = lax.dynamic_index_in_dim(stash_slots[0], wanted_slot, 0, keepdims=False)
    weight = out_proj[0]
    rows_all = residual.shape[1]
    evicted, stored = shifted((attn_in[0], request), "pipe", half_way)
    context = attend(attn_in[0])
    rows_share = rows_all // lax.axis_size("tensor")
    summed = summed_on_arrival(
        jnp.dot(context, weight, preferred_element_type=jnp.float32), "tensor", 0
    )
    own_rows = lax.dynamic_slice_in_dim(
        residual[0], lax.axis_index("tensor") * rows_share, rows_share, 0
    )
    share_out = (own_rows.astype(jnp.float32) + summed).astype(jnp.bfloat16)
    moved = shifted(share_out, "pipe", 1)
    arrived = gathered_copies(moved, "tensor", 0)
    fwd_out = arrived[None]
    grad_context = lax.dot_general(
        grad_in[0], weight, (((1,), (1,)), ((), ())), preferred_element_type=jnp.float32
    )
    qkv_grad = attend_back(stored, grad_context.astype(jnp.bfloat16))[None]
    return (fwd_out, qkv_grad, evicted[None])


def solution(mesh):
    in_specs = (
        P("pipe", None, None),
        P("pipe", "tensor", None),
        P("pipe", None, None, "tensor"),
        P("pipe", None, None, None, "tensor"),
        P("pipe", None, None),
        P(),
    )
    out_specs = (
        P("pipe", None, None),
        P("pipe", None, None, "tensor"),
        P("pipe", None, None, "tensor"),
    )
    return jax.shard_map(
        on_device, mesh=mesh, in_specs=in_specs, out_specs=out_specs, check_vma=False
    )
```

profile of v0, /device:TPU:1, one launch (start us, length us, event | category | flops | bytes accessed | tf_op | source)
XLA Modules:
  0.0 94.6 jit_solution(5634927722433662192)
XLA Ops:
  0.6 0.0 copy-start
  0.7 1.1 %fusion.29 = (bf16[1,1,128,256]{3,2,1,0:T(8,128)(2,1)S(1)}, bf16[1,1,128,256]{3,2,1,0:T(8,128)(2,1)S(1)}, bf16[1,1,128,256]{3,2,1,0:T(8,128)(2,1)S(1)}) fusion(bf16[1,3,128,256]{3,2,1,0:T(8,128)(2,1)} %param.8), kind=kLoop, calls=%fused_computation.40 | loop fusion | bytes 393216 | tf_op jit(solution)/shard_map/slice | solution.py:58
  1.7 0.1 copy.54
  1.9 0.1 copy.55
  2.0 0.3 fusion.30
  2.3 0.1 copy.56
  2.4 0.2 fusion.21
  2.6 0.1 copy.27
  2.8 0.0 copy-done
  2.8 1.7 %fusion.3 = f32[16,8,4096]{2,1,0:T(8,128)} fusion(bf16[16,8,256]{2,1,0:T(8,128)(2,1)S(1)} %convert_element_type.56, bf16[1,256,4096]{2,1,0:T(8,128)(2,1)S(1)} %copy-done), kind=kOutput, calls=%fused_computation.3 | convolution fusion | flops 268435456 | bytes 4259840 | tf_op jit(solution)/shard_map/dot_general | solution.py:96
  4.5 0.0 copy-start.3
  4.5 0.0 copy-start.1
  4.5 18.4 %all-to-all-start = ((f32[16,8,4096]{2,1,0:T(8,128)}), f32[16,8,4096]{2,1,0:T(8,128)}, u32[]{:S(2)}, u32[]{:S(2)}) async-start(f32[16,8,4096]{2,1,0:T(8,128)} %fusion.3), calls=%async_computation | async-start | bytes 4194304 | tf_op jit(solution)/shard_map/all_to_all | solution.py:16
  22.9 0.0 copy-done.3
  22.9 0.6 dynamic_slice.12
  25.4 0.9 constant_dynamic-slice_fusion
  26.4 0.8 copy.28
  27.2 1.9 %collective-permute-start.1 = (bf16[3,128,256]{1,2,0:T(8,128)(2,1)}, bf16[3,128,256]{1,2,0:T(8,128)(2,1)S(1)}, u32[]{:S(2)}, u32[]{:S(2)}) collective-permute-start(bf16[3,128,256]{1,2,0:T(8,128)(2,1)} %bitcast.65), channel_id=1, source_target_pairs={{512,0},{528,16},{544,32},{560,48},{576,64},{592,80},{608,96},{624... | collective-permute-start | bytes 589832 | tf_op jit(solution)/shard_map/ppermute | solution.py:23
  29.1 3.4 %collective-permute-start.2 = (bf16[3,128,256]{2,1,0:T(8,128)(2,1)}, bf16[3,128,256]{2,1,0:T(8,128)(2,1)}, u32[]{:S(2)}, u32[]{:S(2)}) collective-permute-start(bf16[3,128,256]{2,1,0:T(8,128)(2,1)} %bitcast.20), channel_id=1, source_target_pairs={{512,0},{528,16},{544,32},{560,48},{576,64},{592,80},{608,96},{624... | collective-permute-start | bytes 589832 | tf_op jit(solution)/shard_map/ppermute | solution.py:23
  32.5 0.0 copy-done.1
  32.5 0.8 fusion.15
  33.4 0.1 copy.57
  33.5 10.9 %collective-permute-done.1 = bf16[3,128,256]{1,2,0:T(8,128)(2,1)S(1)} collective-permute-done((bf16[3,128,256]{1,2,0:T(8,128)(2,1)}, bf16[3,128,256]{1,2,0:T(8,128)(2,1)S(1)}, u32[]{:S(2)}, u32[]{:S(2)}) %collective-permute-start.1) | collective-permute-done | bytes 196640 | tf_op jit(solution)/shard_map/ppermute | solution.py:23
  44.4 0.3 fusion.31
  44.7 0.0 copy-start.2
  44.7 6.8 %all-to-all-done = f32[16,8,4096]{2,1,0:T(8,128)} async-done(((f32[16,8,4096]{2,1,0:T(8,128)}), f32[16,8,4096]{2,1,0:T(8,128)}, u32[]{:S(2)}, u32[]{:S(2)}) %all-to-all-start) | async-done | bytes 2097184 | tf_op jit(solution)/shard_map/all_to_all | solution.py:16
  51.4 1.7 %reduce_sum.37 = f32[8,4096]{1,0:T(8,128)S(1)} reduce(f32[16,8,4096]{2,1,0:T(8,128)} %all-to-all-done, f32[]{:T(128)} %constant.41.clone.1), dimensions={0}, to_apply=%region_2.3 | reduce | flops 491520 | bytes 2228228 | tf_op jit(solution)/shard_map/reduce_sum | solution.py:17
  53.1 0.9 fusion.25
  54.0 1.9 %collective-permute-start = (bf16[8,4096]{1,0:T(8,128)(2,1)S(1)}, bf16[8,4096]{1,0:T(8,128)(2,1)S(1)}, u32[]{:S(2)}, u32[]{:S(2)}) collective-permute-start(bf16[8,4096]{1,0:T(8,128)(2,1)S(1)} %fusion.25), channel_id=1, source_target_pairs={{1008,0},{0,16},{16,32},{32,48},{48,64},{64,80},{80,96},{96,112},{... | collective-permute-start | bytes 196616 | tf_op jit(solution)/shard_map/ppermute | solution.py:23
  55.9 8.3 %collective-permute-done = bf16[8,4096]{1,0:T(8,128)(2,1)S(1)} collective-permute-done((bf16[8,4096]{1,0:T(8,128)(2,1)S(1)}, bf16[8,4096]{1,0:T(8,128)(2,1)S(1)}, u32[]{:S(2)}, u32[]{:S(2)}) %collective-permute-start) | collective-permute-done | bytes 65568 | tf_op jit(solution)/shard_map/ppermute | solution.py:23
  64.2 1.1 %broadcast_in_dim.24 = bf16[16,8,4096]{2,1,0:T(8,128)(2,1)} broadcast(bf16[8,4096]{1,0:T(8,128)(2,1)S(1)} %collective-permute-done), dimensions={1,2} | broadcast | bytes 1114112 | tf_op jit(solution)/shard_map/broadcast_in_dim | solution.py:35
  65.3 0.0 copy-done.2
  65.3 9.8 %all-to-all-start.1 = ((bf16[16,8,4096]{2,1,0:T(8,128)(2,1)}), bf16[16,8,4096]{2,1,0:T(8,128)(2,1)S(1)}, u32[]{:S(2)}, u32[]{:S(2)}) async-start(bf16[16,8,4096]{2,1,0:T(8,128)(2,1)} %broadcast_in_dim.24), calls=%async_computation.1 | async-start | bytes 2097152 | tf_op jit(solution)/shard_map/all_to_all | solution.py:34
  75.1 1.2 %fusion.18 = bf16[2,128,128]{1,2,0:T(8,128)(2,1)S(1)} fusion(f32[2,128,128]{1,2,0:T(8,128)} %copy-done.2, f32[2,128]{1,0:T(2,128)S(1)} %get-tuple-element.14, bf16[128,2,128]{0,2,1:T(8,128)(2,1)S(1)} %bitcast.55, bf16[128,2,128]{0,2,1:T(8,128)(2,1)S(1)} %bitcast.68), kind=kOutput, calls=%fused_computation.20 | convolution fusion | flops 16974208 | bytes 328704 | tf_op jit(solution)/shard_map/sub | solution.py:73
  76.3 0.2 fusion.22
  76.5 0.2 fusion.23
  76.7 0.2 convolution_convert_fusion
  76.9 0.1 copy.38
  77.0 0.7 copy.35
  77.8 0.9 pad_maximum_fusion
  78.6 0.8 copy.41
  79.5 0.0 collective-permute-done.2
  79.5 12.6 %all-to-all-done.1 = bf16[16,8,4096]{2,1,0:T(8,128)(2,1)S(1)} async-done(((bf16[16,8,4096]{2,1,0:T(8,128)(2,1)}), bf16[16,8,4096]{2,1,0:T(8,128)(2,1)S(1)}, u32[]{:S(2)}, u32[]{:S(2)}) %all-to-all-start.1) | async-done | bytes 1048608 | tf_op jit(solution)/shard_map/all_to_all | solution.py:34
  92.0 1.0 %copy.60 = bf16[1,128,4096]{2,1,0:T(8,128)(2,1)} copy(bf16[1,128,4096]{2,1,0:T(8,128)(2,1)S(1)} %bitcast.54) | data formatting | bytes 2097152
  93.0 1.6 %copy.61 = bf16[1,3,128,256]{3,2,1,0:T(8,128)(2,1)} copy(bf16[1,3,128,256]{3,2,1,0:T(8,128)(2,1)} %bitcast.21) | data formatting | bytes 393216
  (5 shorter events, 0.1 us)
Async XLA Ops:
  0.6 2.1 %copy-start = (bf16[1,256,4096]{2,1,0:T(8,128)(2,1)S(1)}, bf16[1,256,4096]{2,1,0:T(8,128)(2,1)}, u32[]{:S(2)}) copy-start(bf16[1,256,4096]{2,1,0:T(8,128)(2,1)} %param.7) | copy-start | bytes 6291460
  4.5 18.4 %copy-start.3 = (s32[64]{0:T(128)S(1)}, s32[64]{0:T(128)}, u32[]{:S(2)}) copy-start(s32[64]{0:T(128)} %param.11) | copy-start | bytes 772
  4.5 28.0 %copy-start.1 = (bf16[1,128,4096]{2,1,0:T(8,128)(2,1)S(1)}, bf16[1,128,4096]{2,1,0:T(8,128)(2,1)}, u32[]{:S(2)}) copy-start(bf16[1,128,4096]{2,1,0:T(8,128)(2,1)} %param.10) | copy-start | bytes 3145732
  4.5 46.9 %all-to-all-start = ((f32[16,8,4096]{2,1,0:T(8,128)}), f32[16,8,4096]{2,1,0:T(8,128)}, u32[]{:S(2)}, u32[]{:S(2)}) async-start(f32[16,8,4096]{2,1,0:T(8,128)} %fusion.3), calls=%async_computation | async-start | bytes 4194304 | tf_op jit(solution)/shard_map/all_to_all | solution.py:16
  27.2 17.2 %collective-permute-start.1 = (bf16[3,128,256]{1,2,0:T(8,128)(2,1)}, bf16[3,128,256]{1,2,0:T(8,128)(2,1)S(1)}, u32[]{:S(2)}, u32[]{:S(2)}) collective-permute-start(bf16[3,128,256]{1,2,0:T(8,128)(2,1)} %bitcast.65), channel_id=1, source_target_pairs={{512,0},{528,16},{544,32},{560,48},{576,64},{592,80},{608,96},{624... | collective-permute-start | bytes 589832 | tf_op jit(solution)/shard_map/ppermute | solution.py:23
  29.1 50.4 %collective-permute-start.2 = (bf16[3,128,256]{2,1,0:T(8,128)(2,1)}, bf16[3,128,256]{2,1,0:T(8,128)(2,1)}, u32[]{:S(2)}, u32[]{:S(2)}) collective-permute-start(bf16[3,128,256]{2,1,0:T(8,128)(2,1)} %bitcast.20), channel_id=1, source_target_pairs={{512,0},{528,16},{544,32},{560,48},{576,64},{592,80},{608,96},{624... | collective-permute-start | bytes 589832 | tf_op jit(solution)/shard_map/ppermute | solution.py:23
  44.7 20.6 %copy-start.2 = (f32[2,128,128]{1,2,0:T(8,128)}, f32[2,128,128]{1,2,0:T(8,128)S(1)}, u32[]{:S(2)}) copy-start(f32[2,128,128]{1,2,0:T(8,128)S(1)} %get-tuple-element.15) | copy-start | bytes 393220
  54.0 10.2 %collective-permute-start = (bf16[8,4096]{1,0:T(8,128)(2,1)S(1)}, bf16[8,4096]{1,0:T(8,128)(2,1)S(1)}, u32[]{:S(2)}, u32[]{:S(2)}) collective-permute-start(bf16[8,4096]{1,0:T(8,128)(2,1)S(1)} %fusion.25), channel_id=1, source_target_pairs={{1008,0},{0,16},{16,32},{32,48},{48,64},{64,80},{80,96},{96,112},{... | collective-permute-start | bytes 196616 | tf_op jit(solution)/shard_map/ppermute | solution.py:23
  65.3 26.8 %all-to-all-start.1 = ((bf16[16,8,4096]{2,1,0:T(8,128)(2,1)}), bf16[16,8,4096]{2,1,0:T(8,128)(2,1)S(1)}, u32[]{:S(2)}, u32[]{:S(2)}) async-start(bf16[16,8,4096]{2,1,0:T(8,128)(2,1)} %broadcast_in_dim.24), calls=%async_computation.1 | async-start | bytes 2097152 | tf_op jit(solution)/shard_map/all_to_all | solution.py:34
where the time goes:
time: 95.2 us; the launch traced here: 94.6 us
  waiting for transfers between devices  38.5 us (40%)
  starting transfers between devices  35.4 us (37%)
  local copies, waits for them, and re-layouts  9.37 us (10%)
  matrix products  5.13 us (5%)
  other arithmetic  3.48 us (4%)
  between operations  2.76 us (3%)
    ppermute x3, waiting for transfers between devices, shifted(): return lax.ppermute(block, axis, route)  19.2 us
    all_to_all x1, starting transfers between devices, summed_on_arrival(): lax.all_to_all(cut_along(value, dim, count), axis, 0, 0, tiled=True)  18.4 us
    all_to_all x1, waiting for transfers between devices, sent_to_all(): lax.all_to_all(jnp.broadcast_to(value[None], (count, *value.shape)), axis...  12.6 us
    all_to_all x1, starting transfers between devices, sent_to_all(): lax.all_to_all(jnp.broadcast_to(value[None], (count, *value.shape)), axis...  9.8 us
    ppermute x3, starting transfers between devices, shifted(): return lax.ppermute(block, axis, route)  7.19 us
    all_to_all x1, waiting for transfers between devices, summed_on_arrival(): lax.all_to_all(cut_along(value, dim, count), axis, 0, 0, tiled=True)  6.75 us
    unnamed x14, local copies, waits for them, and re-layouts  3.77 us
  transfers between devices with their start and end apart: 5, of which 4 were waited for; matrix products, arithmetic and copies ran while one was open for 12% of the time, Pallas kernels for 0%

commit v1 on v0

v1 whole, which is shorter than its diff:
```python
import jax
import jax.numpy as jnp
from jax import lax
from jax.experimental import pallas as pl
from jax.experimental.pallas import tpu as pltpu
from jax.sharding import PartitionSpec as P


HD = 128
SCALE = HD ** (-0.5)
BF = jnp.bfloat16
F32 = jnp.float32
VMEM = pl.BlockSpec(memory_space=pltpu.VMEM)
SMEM = pl.BlockSpec(memory_space=pltpu.SMEM)
ANY = pl.BlockSpec(memory_space=pl.ANY)


def struct(shape, dtype=BF):
    return jax.ShapeDtypeStruct(shape, dtype)


def dot(a, b, ca, cb):
    return lax.dot_general(a, b, (((ca,), (cb,)), ((), ())), preferred_element_type=F32)


def probs_of(query, key):
    scores = dot(query, key, 1, 1) * SCALE
    rows = lax.broadcasted_iota(jnp.int32, scores.shape, 0)
    cols = lax.broadcasted_iota(jnp.int32, scores.shape, 1)
    scores = jnp.where(rows >= cols, scores, -jnp.inf)
    top = jnp.max(scores, axis=1, keepdims=True)
    weights = jnp.exp(scores - top)
    return weights / jnp.sum(weights, axis=1, keepdims=True)


def forward_kernel(qkv_hbm, weight_hbm, out_hbm, qkv, weight, out, sems):
    tiles, tile = weight.shape[0], weight.shape[2]
    head_count = qkv.shape[2] // HD
    load_qkv = pltpu.make_async_copy(qkv_hbm.at[0], qkv, sems.at[0])
    loads, stores = [], []
    for n in range(tiles):
        c = slice(n * tile, (n + 1) * tile)
        loads.append(pltpu.make_async_copy(weight_hbm.at[0, :, c], weight.at[n], sems.at[1 + n]))
        stores.append(pltpu.make_async_copy(out.at[n], out_hbm.at[:, c], sems.at[1 + tiles + n]))
    load_qkv.start()
    for load in loads:
        load.start()
    load_qkv.wait()
    heads = []
    for h in range(head_count):
        c = slice(h * HD, (h + 1) * HD)
        probs = probs_of(qkv[0, :, c], qkv[1, :, c]).astype(BF)
        heads.append(dot(probs, qkv[2, :, c], 1, 0).astype(BF))
    context = jnp.concatenate(heads, axis=1)
    for n in range(tiles):
        loads[n].wait()
        out[n] = dot(context, weight[n], 1, 0).astype(BF)
        stores[n].start()
    for store in stores:
        store.wait()


def pick_kernel(slots, stash, qkv, residual, pair, rows, sems):
    sections = lax.axis_size("pipe")
    partner = lax.rem(lax.axis_index("pipe") + sections // 2, sections)
    share = rows.shape[0]
    first = pl.multiple_of(lax.axis_index("tensor") * share, share)
    copies = (
        pltpu.make_async_copy(stash.at[0, slots[partner]], pair.at[0], sems.at[0]),
        pltpu.make_async_copy(qkv.at[0], pair.at[1], sems.at[1]),
        pltpu.make_async_copy(residual.at[0, pl.ds(first, share)], rows, sems.at[2]),
    )
    for copy in copies:
        copy.start()
    for copy in copies:
        copy.wait()


def backward_kernel(pair, grad_context, grads, evicted):
    for h in range(grad_context.shape[1] // HD):
        c = slice(h * HD, (h + 1) * HD)
        query, key, value = pair[0, 0, :, c], pair[0, 1, :, c], pair[0, 2, :, c]
        grad = grad_context[:, c]
        probs = probs_of(query, key)
        grad_probs = dot(grad, value, 1, 1)
        delta = jnp.sum(probs * grad_probs, axis=1, keepdims=True)
        grad_scores = (probs * (grad_probs - delta)).astype(BF)
        grads[0, 0, :, c] = (dot(grad_scores, key, 1, 0) * SCALE).astype(BF)
        grads[0, 1, :, c] = (dot(grad_scores, query, 0, 0) * SCALE).astype(BF)
        grads[0, 2, :, c] = dot(probs.astype(BF), grad, 0, 0).astype(BF)
    evicted[0] = pair[1]


def shifted(block, axis, distance):
    count = lax.axis_size(axis)
    return lax.ppermute(block, axis, [((i - distance) % count, i) for i in range(count)])


def step(residual, out_proj, attn_in, stash_slots, grad_in, stash_slot):
    sections, members = lax.axis_size("pipe"), lax.axis_size("tensor")
    weight = out_proj[0]
    rows, width = residual.shape[1:]
    share = rows // members
    tiles = 4
    partial = pl.pallas_call(
        forward_kernel,
        out_shape=struct((rows, width)),
        in_specs=[ANY, ANY],
        out_specs=ANY,
        scratch_shapes=[
            pltpu.VMEM(attn_in.shape[1:], BF),
            pltpu.VMEM((tiles, weight.shape[0], width // tiles), BF),
            pltpu.VMEM((tiles, rows, width // tiles), BF),
            pltpu.SemaphoreType.DMA((1 + 2 * tiles,)),
        ],
        name="front",
    )(attn_in, out_proj)
    parts = lax.all_to_all(partial.reshape(members, share, width), "tensor", 0, 0, tiled=True)
    pair, own_rows = pl.pallas_call(
        pick_kernel,
        out_shape=(struct((2, *attn_in.shape[1:])), struct((share, width))),
        in_specs=[SMEM, ANY, ANY, ANY],
        out_specs=(VMEM, VMEM),
        scratch_shapes=[pltpu.SemaphoreType.DMA((3,))],
        name="pick",
    )(stash_slot, stash_slots, attn_in, residual)
    swapped = shifted(pair, "pipe", sections // 2)
    grad_context = dot(grad_in[0], weight, 1, 1).astype(BF)
    own = (own_rows.astype(F32) + jnp.sum(parts.astype(F32), axis=0)).astype(BF)
    moved = shifted(own, "pipe", 1)
    copies = jnp.broadcast_to(moved[None], (members, share, width))
    arrived = lax.all_to_all(copies, "tensor", 0, 0, tiled=True)
    qkv_grad, evicted = pl.pallas_call(
        backward_kernel,
        out_shape=(struct(attn_in.shape), struct(attn_in.shape)),
        in_specs=[VMEM, VMEM],
        out_specs=(VMEM, VMEM),
        name="back",
        compiler_params=pltpu.CompilerParams(vmem_limit_bytes=4 << 20),
    )(swapped, grad_context)
    return arrived.reshape(1, rows, width), qkv_grad, evicted


def solution(mesh):
    in_specs = (
        P("pipe", None, None),
        P("pipe", "tensor", None),
        P("pipe", None, None, "tensor"),
        P("pipe", None, None, None, "tensor"),
        P("pipe", None, None),
        P(),
    )
    out_specs = (
        P("pipe", None, None),
        P("pipe", None, None, "tensor"),
        P("pipe", None, None, "tensor"),
    )
    return jax.shard_map(step, mesh=mesh, in_specs=in_specs, out_specs=out_specs, check_vma=False)
```

time: 95.2 us -> 85.5 us (0.90)
  Pallas kernels: 0 us -> 7.73 us
  starting transfers between devices: 35.4 us -> 29.2 us
  local copies, waits for them, and re-layouts: 9.37 us -> 3.38 us
  matrix products: 5.13 us -> 0.83 us
  waiting for transfers between devices: 38.5 us -> 41 us
  between operations: 2.76 us -> 0.72 us
  other arithmetic: 3.48 us -> 2.23 us
    pallas_call x0 -> x3, Pallas kernels: none -> 7.73 us  [the longest x1 3.51 us: step(): pl.pallas_call(forward_kernel, out_shape=struct((rows, width)), in_specs=...]
    ppermute x3 -> x2, waiting for transfers between devices: 19.2 us -> 26.3 us  [shifted(): lax.ppermute(block, axis, [((i - distance) % count, i) for i in range(cou...]
    all_to_all x2, waiting for transfers between devices: 19.3 us -> 14.7 us  [the longest x1 14.7 us: step(): lax.all_to_all(partial.reshape(members, share, width), 'tensor', 0, 0, ti...]
    all_to_all x2, starting transfers between devices: 28.2 us -> 24.3 us  [the longest x1 18.2 us: step(): lax.all_to_all(partial.reshape(members, share, width), 'tensor', 0, 0, ti...]
    dot_general x6 -> x1, matrix products: 3.36 us -> 0.83 us  [dot(): lax.dot_general(a, b, (((ca,), (cb,)), ((), ())), preferred_element_type=...]
    dynamic_slice x3 -> x0, local copies, waits for them, and re-layouts: 2.35 us -> none  [the longest x2 1.76 us: on_device(): lax.dynamic_index_in_dim(stash_slots[0], wanted_slot, 0, keepdims=False)]
    ppermute x3 -> x2, starting transfers between devices: 7.19 us -> 4.9 us  [shifted(): lax.ppermute(block, axis, [((i - distance) % count, i) for i in range(cou...]
    sub x3 -> x0, matrix products: 1.77 us -> none  [the longest x1 1.22 us: attend_back(): grad_scores = (attn_probs * (grad_probs - row_delta)).astype(jnp.bfloat16)]
  transfers between devices with their start and end apart: 5 -> 4, of which waited for: 4 -> 3; matrix products, arithmetic and copies ran while one was open for 12% -> 1% of each run, Pallas kernels for 0% -> 5%
where the time goes in v1:
time: 85.5 us; the launch traced here: 85 us
  waiting for transfers between devices  41 us (48%)
  starting transfers between devices  29.2 us (34%)
  Pallas kernels  7.73 us (9%)
  local copies, waits for them, and re-layouts  3.38 us (4%)
  other arithmetic  2.23 us (3%)
    ppermute x2, waiting for transfers between devices, shifted(): lax.ppermute(block, axis, [((i - distance) % count, i) for i in range(cou...  26.3 us
    all_to_all x1, starting transfers between devices, step(): lax.all_to_all(partial.reshape(members, share, width), 'tensor', 0, 0, ti...  18.2 us
    all_to_all x1, waiting for transfers between devices, step(): lax.all_to_all(partial.reshape(members, share, width), 'tensor', 0, 0, ti...  14.7 us
    all_to_all x1, starting transfers between devices, step(): arrived = lax.all_to_all(copies, 'tensor', 0, 0, tiled=True)  6.05 us
    ppermute x2, starting transfers between devices, shifted(): lax.ppermute(block, axis, [((i - distance) % count, i) for i in range(cou...  4.9 us
    pallas_call x1, Pallas kernels, step(): pl.pallas_call(forward_kernel, out_shape=struct((rows, width)), in_specs=...  3.51 us
    pallas_call x1, Pallas kernels, step(): pl.pallas_call(pick_kernel, out_shape=(struct((2, *attn_in.shape[1:])), s...  2.5 us
    unnamed x7, local copies, waits for them, and re-layouts  2.31 us
  transfers between devices with their start and end apart: 4, of which 3 were waited for; matrix products, arithmetic and copies ran while one was open for 1% of the time, Pallas kernels for 5%

profile of v1, /device:TPU:1, one launch (start us, length us, event | category | flops | bytes accessed | tf_op | source)
XLA Modules:
  0.0 85.0 jit_solution(18170941687363612632)
XLA Ops:
  0.6 0.0 copy-start
  0.6 3.5 %front.1 = bf16[128,4096]{1,0:T(8,128)(2,1)} custom-call(bf16[1,3,128,256]{3,2,1,0:T(8,128)(2,1)} %qkv_hbm.1, bf16[1,256,4096]{2,1,0:T(8,128)(2,1)} %weight_hbm.1), custom_call_target="tpu_custom_call" | custom-call | tf_op jit(solution)/shard_map/front/pallas_call | solution.py:105
  4.2 18.2 %all-to-all-start = ((bf16[16,8,4096]{2,1,0:T(8,128)(2,1)}), bf16[16,8,4096]{2,1,0:T(8,128)(2,1)}, u32[]{:S(2)}, u32[]{:S(2)}) async-start(bf16[16,8,4096]{2,1,0:T(8,128)(2,1)} %bitcast.10), calls=%async_computation | async-start | bytes 2097152 | tf_op jit(solution)/shard_map/all_to_all | solution.py:118
  22.4 2.5 %pick.1 = (bf16[2,3,128,256]{3,2,1,0:T(8,128)(2,1)}, bf16[8,4096]{1,0:T(8,128)(2,1)}) custom-call(s32[64]{0:T(128)} %slots.1, bf16[1,2,3,128,256]{4,3,2,1,0:T(8,128)(2,1)} %stash.1, bf16[1,3,128,256]{3,2,1,0:T(8,128)(2,1)} %qkv_hbm.1, bf16[1,128,4096]{2,1,0:T(8,128)(2,1)} %residual.1), custom_call_target="tpu_custom_call" | custom-call | tf_op jit(solution)/shard_map/pick/pallas_call | solution.py:119
  24.9 0.0 copy-start.2
  24.9 0.0 copy-start.1
  24.9 14.7 %all-to-all-done = bf16[16,8,4096]{2,1,0:T(8,128)(2,1)} async-done(((bf16[16,8,4096]{2,1,0:T(8,128)(2,1)}), bf16[16,8,4096]{2,1,0:T(8,128)(2,1)}, u32[]{:S(2)}, u32[]{:S(2)}) %all-to-all-start) | async-done | bytes 1048608 | tf_op jit(solution)/shard_map/all_to_all | solution.py:118
  39.6 1.4 %convert_reduce_fusion = f32[8,4096]{1,0:T(8,128)S(1)} fusion(bf16[16,8,4096]{2,1,0:T(8,128)(2,1)} %all-to-all-done), kind=kLoop, calls=%fused_computation.2 | loop fusion | flops 1015808 | bytes 1179648 | tf_op jit(solution)/shard_map/reduce_sum | solution.py:129
  40.9 0.9 %add_convert_fusion = bf16[8,4096]{1,0:T(8,128)(2,1)S(1)} fusion(f32[8,4096]{1,0:T(8,128)S(1)} %convert_reduce_fusion, bf16[8,4096]{1,0:T(8,128)(2,1)} %get-tuple-element.7), kind=kLoop, calls=%fused_computation.5 | loop fusion | flops 98304 | bytes 262144 | tf_op jit(solution)/shard_map/convert_element_type | solution.py:129
  41.8 1.9 %collective-permute-start = (bf16[8,4096]{1,0:T(8,128)(2,1)S(1)}, bf16[8,4096]{1,0:T(8,128)(2,1)S(1)}, u32[]{:S(2)}, u32[]{:S(2)}) collective-permute-start(bf16[8,4096]{1,0:T(8,128)(2,1)S(1)} %add_convert_fusion), channel_id=1, source_target_pairs={{1008,0},{0,16},{16,32},{32,48},{48,64},{64,80},{80,96},{96,112},{... | collective-permute-start | bytes 196616 | tf_op jit(solution)/shard_map/ppermute | solution.py:96
  43.7 8.3 %collective-permute-done = bf16[8,4096]{1,0:T(8,128)(2,1)S(1)} collective-permute-done((bf16[8,4096]{1,0:T(8,128)(2,1)S(1)}, bf16[8,4096]{1,0:T(8,128)(2,1)S(1)}, u32[]{:S(2)}, u32[]{:S(2)}) %collective-permute-start) | collective-permute-done | bytes 65568 | tf_op jit(solution)/shard_map/ppermute | solution.py:96
  52.1 1.1 %broadcast_in_dim.2 = bf16[16,8,4096]{2,1,0:T(8,128)(2,1)} broadcast(bf16[8,4096]{1,0:T(8,128)(2,1)S(1)} %collective-permute-done), dimensions={1,2} | broadcast | bytes 1114112 | tf_op jit(solution)/shard_map/broadcast_in_dim | solution.py:131
  53.1 6.0 %all-to-all-start.1 = ((bf16[16,8,4096]{2,1,0:T(8,128)(2,1)}), bf16[16,8,4096]{2,1,0:T(8,128)(2,1)}, u32[]{:S(2)}, u32[]{:S(2)}) async-start(bf16[16,8,4096]{2,1,0:T(8,128)(2,1)} %broadcast_in_dim.2), calls=%async_computation.1 | async-start | bytes 2097152 | tf_op jit(solution)/shard_map/all_to_all | solution.py:132
  59.2 0.0 copy-done.2
  59.2 3.0 %collective-permute-start.1 = (bf16[2,3,128,256]{3,2,1,0:T(8,128)(2,1)S(1)}, bf16[2,3,128,256]{3,2,1,0:T(8,128)(2,1)S(1)}, u32[]{:S(2)}, u32[]{:S(2)}) collective-permute-start(bf16[2,3,128,256]{3,2,1,0:T(8,128)(2,1)S(1)} %copy-done.2), channel_id=1, source_target_pairs={{512,0},{528,16},{544,32},{560,48},{576,64},{592,80},{608,96},{624... | collective-permute-start | bytes 1179656 | tf_op jit(solution)/shard_map/ppermute | solution.py:96
  62.2 0.0 copy-done
  62.2 0.0 copy-done.1
  62.2 0.8 fusion.2.grad_context
  63.0 18.0 %collective-permute-done.1.pair = bf16[2,3,128,256]{3,2,1,0:T(8,128)(2,1)S(1)} collective-permute-done((bf16[2,3,128,256]{3,2,1,0:T(8,128)(2,1)S(1)}, bf16[2,3,128,256]{3,2,1,0:T(8,128)(2,1)S(1)}, u32[]{:S(2)}, u32[]{:S(2)}) %collective-permute-start.1) | collective-permute-done | bytes 393248 | tf_op jit(solution)/shard_map/ppermute | solution.py:96
  81.0 1.7 %back.1 = (bf16[1,3,128,256]{3,2,1,0:T(8,128)(2,1)}, bf16[1,3,128,256]{3,2,1,0:T(8,128)(2,1)}) custom-call(bf16[2,3,128,256]{3,2,1,0:T(8,128)(2,1)S(1)} %collective-permute-done.1.pair, bf16[128,256]{1,0:T(8,128)(2,1)S(1)} %fusion.2.grad_context), custom_call_target="tpu_custom_call" | custom-call | tf_op jit(solution)/shard_map/back/pallas_call | solution.py:133
  82.7 0.0 all-to-all-done.1
  82.7 2.3 %copy.10 = bf16[1,128,4096]{2,1,0:T(8,128)(2,1)} copy(bf16[1,128,4096]{2,1,0:T(8,128)(2,1)} %bitcast.1) | data formatting | bytes 2097152
Async XLA Ops:
  0.6 61.5 %copy-start = (bf16[1,128,4096]{2,1,0:T(8,128)(2,1)S(1)}, bf16[1,128,4096]{2,1,0:T(8,128)(2,1)}, u32[]{:S(2)}) copy-start(bf16[1,128,4096]{2,1,0:T(8,128)(2,1)} %param.10) | copy-start | bytes 3145732
  4.2 35.4 %all-to-all-start = ((bf16[16,8,4096]{2,1,0:T(8,128)(2,1)}), bf16[16,8,4096]{2,1,0:T(8,128)(2,1)}, u32[]{:S(2)}, u32[]{:S(2)}) async-start(bf16[16,8,4096]{2,1,0:T(8,128)(2,1)} %bitcast.10), calls=%async_computation | async-start | bytes 2097152 | tf_op jit(solution)/shard_map/all_to_all | solution.py:118
  24.9 34.3 %copy-start.2 = (bf16[2,3,128,256]{3,2,1,0:T(8,128)(2,1)S(1)}, bf16[2,3,128,256]{3,2,1,0:T(8,128)(2,1)}, u32[]{:S(2)}) copy-start(bf16[2,3,128,256]{3,2,1,0:T(8,128)(2,1)} %get-tuple-element.8) | copy-start | bytes 1179652
  24.9 37.3 %copy-start.1 = (bf16[1,256,4096]{2,1,0:T(8,128)(2,1)S(1)}, bf16[1,256,4096]{2,1,0:T(8,128)(2,1)}, u32[]{:S(2)}) copy-start(bf16[1,256,4096]{2,1,0:T(8,128)(2,1)} %weight_hbm.1) | copy-start | bytes 6291460
  41.8 10.3 %collective-permute-start = (bf16[8,4096]{1,0:T(8,128)(2,1)S(1)}, bf16[8,4096]{1,0:T(8,128)(2,1)S(1)}, u32[]{:S(2)}, u32[]{:S(2)}) collective-permute-start(bf16[8,4096]{1,0:T(8,128)(2,1)S(1)} %add_convert_fusion), channel_id=1, source_target_pairs={{1008,0},{0,16},{16,32},{32,48},{48,64},{64,80},{80,96},{96,112},{... | collective-permute-start | bytes 196616 | tf_op jit(solution)/shard_map/ppermute | solution.py:96
  53.1 29.6 %all-to-all-start.1 = ((bf16[16,8,4096]{2,1,0:T(8,128)(2,1)}), bf16[16,8,4096]{2,1,0:T(8,128)(2,1)}, u32[]{:S(2)}, u32[]{:S(2)}) async-start(bf16[16,8,4096]{2,1,0:T(8,128)(2,1)} %broadcast_in_dim.2), calls=%async_computation.1 | async-start | bytes 2097152 | tf_op jit(solution)/shard_map/all_to_all | solution.py:132
  59.2 21.8 %collective-permute-start.1 = (bf16[2,3,128,256]{3,2,1,0:T(8,128)(2,1)S(1)}, bf16[2,3,128,256]{3,2,1,0:T(8,128)(2,1)S(1)}, u32[]{:S(2)}, u32[]{:S(2)}) collective-permute-start(bf16[2,3,128,256]{3,2,1,0:T(8,128)(2,1)S(1)} %copy-done.2), channel_id=1, source_target_pairs={{512,0},{528,16},{544,32},{560,48},{576,64},{592,80},{608,96},{624... | collective-permute-start | bytes 1179656 | tf_op jit(solution)/shard_map/ppermute | solution.py:96

commit v2 on v1

--- a/solution.py
+++ b/solution.py
@@ -1,3 +1,5 @@
+import functools
+
 import jax
 import jax.numpy as jnp
 from jax import lax
@@ -13,6 +15,7 @@
 VMEM = pl.BlockSpec(memory_space=pltpu.VMEM)
 SMEM = pl.BlockSpec(memory_space=pltpu.SMEM)
 ANY = pl.BlockSpec(memory_space=pl.ANY)
+SMALL = pltpu.CompilerParams(vmem_limit_bytes=4 << 20)
 
 
 def struct(shape, dtype=BF):
@@ -21,6 +24,10 @@
 
 def dot(a, b, ca, cb):
     return lax.dot_general(a, b, (((ca,), (cb,)), ((), ())), preferred_element_type=F32)
+
+
+def core_of_chip():
+    return lax.rem(lax.axis_index("tensor"), 2)
 
 
 def probs_of(query, key):
@@ -33,9 +40,9 @@
     return weights / jnp.sum(weights, axis=1, keepdims=True)
 
 
-def forward_kernel(qkv_hbm, weight_hbm, out_hbm, qkv, weight, out, sems):
+def forward_kernel(qkv_hbm, weight_hbm, own_context, out_hbm, qkv, weight, context, out, sems):
     tiles, tile = weight.shape[0], weight.shape[2]
-    head_count = qkv.shape[2] // HD
+    half = own_context.shape[0]
     load_qkv = pltpu.make_async_copy(qkv_hbm.at[0], qkv, sems.at[0])
     loads, stores = [], []
     for n in range(tiles):
@@ -46,15 +53,16 @@
     for load in loads:
         load.start()
     load_qkv.wait()
-    heads = []
-    for h in range(head_count):
+    for h in range(qkv.shape[2] // HD):
         c = slice(h * HD, (h + 1) * HD)
         probs = probs_of(qkv[0, :, c], qkv[1, :, c]).astype(BF)
-        heads.append(dot(probs, qkv[2, :, c], 1, 0).astype(BF))
-    context = jnp.concatenate(heads, axis=1)
+        context[:, c] = dot(probs, qkv[2, :, c], 1, 0).astype(BF)
+    core = core_of_chip()
+    own_context[...] = context[pl.ds(pl.multiple_of(core * half, half), half), :]
+    theirs = context[pl.ds(pl.multiple_of((1 - core) * half, half), half), :]
     for n in range(tiles):
         loads[n].wait()
-        out[n] = dot(context, weight[n], 1, 0).astype(BF)
+        out[n] = dot(theirs, weight[n], 1, 0).astype(BF)
         stores[n].start()
     for store in stores:
         store.wait()
@@ -64,7 +72,9 @@
     sections = lax.axis_size("pipe")
     partner = lax.rem(lax.axis_index("pipe") + sections // 2, sections)
     share = rows.shape[0]
-    first = pl.multiple_of(lax.axis_index("tensor") * share, share)
+    half = residual.shape[1] // 2
+    first = core_of_chip() * half + lax.div(lax.axis_index("tensor"), 2) * share
+    first = pl.multiple_of(first, share)
     copies = (
         pltpu.make_async_copy(stash.at[0, slots[partner]], pair.at[0], sems.at[0]),
         pltpu.make_async_copy(qkv.at[0], pair.at[1], sems.at[1]),
@@ -74,6 +84,16 @@
         copy.start()
     for copy in copies:
         copy.wait()
+
+
+def place_kernel(other, block, *refs):
+    out, sem = refs[-2:]
+    half = block.shape[0]
+    core = core_of_chip()
+    first = pl.multiple_of((1 - core if other else core) * half, half)
+    copy = pltpu.make_async_copy(block, out.at[0, pl.ds(first, half)], sem)
+    copy.start()
+    copy.wait()
 
 
 def backward_kernel(pair, grad_context, grads, evicted):
@@ -96,26 +116,40 @@
     return lax.ppermute(block, axis, [((i - distance) % count, i) for i in range(count)])
 
 
+def crossed(block):
+    return lax.ppermute(block, "tensor", [(i, i ^ 1) for i in range(lax.axis_size("tensor"))])
+
+
+def exchanged(blocks):
+    members = lax.axis_size("tensor")
+    groups = [list(range(core, members, 2)) for core in range(2)]
+    return lax.all_to_all(blocks, "tensor", 0, 0, axis_index_groups=groups, tiled=True)
+
+
 def step(residual, out_proj, attn_in, stash_slots, grad_in, stash_slot):
     sections, members = lax.axis_size("pipe"), lax.axis_size("tensor")
     weight = out_proj[0]
     rows, width = residual.shape[1:]
-    share = rows // members
+    chips, half, share = members // 2, rows // 2, rows // members
     tiles = 4
-    partial = pl.pallas_call(
+    own_context, product = pl.pallas_call(
         forward_kernel,
-        out_shape=struct((rows, width)),
+        out_shape=(struct((half, weight.shape[0])), struct((half, width))),
         in_specs=[ANY, ANY],
-        out_specs=ANY,
+        out_specs=(VMEM, ANY),
         scratch_shapes=[
             pltpu.VMEM(attn_in.shape[1:], BF),
             pltpu.VMEM((tiles, weight.shape[0], width // tiles), BF),
-            pltpu.VMEM((tiles, rows, width // tiles), BF),
+            pltpu.VMEM((rows, weight.shape[0]), BF),
+            pltpu.VMEM((tiles, half, width // tiles), BF),
             pltpu.SemaphoreType.DMA((1 + 2 * tiles,)),
         ],
         name="front",
     )(attn_in, out_proj)
-    parts = lax.all_to_all(partial.reshape(members, share, width), "tensor", 0, 0, tiled=True)
+    received = crossed(product)
+    own = dot(own_context, weight, 1, 0)
+    partial = (own + received.astype(F32)).astype(BF).reshape(chips, share, width)
+    parts = exchanged(partial)
     pair, own_rows = pl.pallas_call(
         pick_kernel,
         out_shape=(struct((2, *attn_in.shape[1:])), struct((share, width))),
@@ -126,19 +160,42 @@
     )(stash_slot, stash_slots, attn_in, residual)
     swapped = shifted(pair, "pipe", sections // 2)
     grad_context = dot(grad_in[0], weight, 1, 1).astype(BF)
-    own = (own_rows.astype(F32) + jnp.sum(parts.astype(F32), axis=0)).astype(BF)
-    moved = shifted(own, "pipe", 1)
-    copies = jnp.broadcast_to(moved[None], (members, share, width))
-    arrived = lax.all_to_all(copies, "tensor", 0, 0, tiled=True)
+    total = own_rows.astype(F32)
+    for chip in range(chips):
+        total = total + parts[chip].astype(F32)
+    total = total.astype(BF)
+    moved = shifted(total, "pipe", 1)
+    copies = jnp.broadcast_to(moved[None], (chips, share, width))
+    arrived = exchanged(copies).reshape(half, width)
     qkv_grad, evicted = pl.pallas_call(
         backward_kernel,
         out_shape=(struct(attn_in.shape), struct(attn_in.shape)),
         in_specs=[VMEM, VMEM],
         out_specs=(VMEM, VMEM),
+        compiler_params=SMALL,
         name="back",
-        compiler_params=pltpu.CompilerParams(vmem_limit_bytes=4 << 20),
     )(swapped, grad_context)
-    return arrived.reshape(1, rows, width), qkv_grad, evicted
+    other = crossed(arrived)
+    placed = pl.pallas_call(
+        functools.partial(place_kernel, False),
+        out_shape=struct(residual.shape),
+        in_specs=[VMEM],
+        out_specs=ANY,
+        scratch_shapes=[pltpu.SemaphoreType.DMA],
+        compiler_params=SMALL,
+        name="place",
+    )(arrived)
+    fwd_out = pl.pallas_call(
+        functools.partial(place_kernel, True),
+        out_shape=struct(residual.shape),
+        in_specs=[VMEM, ANY],
+        out_specs=ANY,
+        input_output_aliases={1: 0},
+        scratch_shapes=[pltpu.SemaphoreType.DMA],
+        compiler_params=SMALL,
+        name="join",
+    )(other, placed)
+    return fwd_out, qkv_grad, evicted
 
 
 def solution(mesh):

time: 85.5 us -> 85.1 us (level)
  waiting for transfers between devices: 41 us -> 27.9 us
  blocking collectives: 0 us -> 12.8 us
  local copies, waits for them, and re-layouts: 3.38 us -> 0.05 us
  Pallas kernels: 7.73 us -> 9.87 us
  matrix products: 0.83 us -> 2.87 us
  other arithmetic: 2.23 us -> 1.18 us
    ppermute x0 -> x2, starting transfers between devices: none -> 21.2 us  [crossed(): lax.ppermute(block, 'tensor', [(i, i ^ 1) for i in range(lax.axis_size('t...]
    all_to_all x2 -> x1, starting transfers between devices: 24.3 us -> 4.14 us  [exchanged(): lax.all_to_all(blocks, 'tensor', 0, 0, axis_index_groups=groups, tiled=True)]
    all_to_all x0 -> x1, blocking collectives: none -> 12.8 us  [exchanged(): lax.all_to_all(blocks, 'tensor', 0, 0, axis_index_groups=groups, tiled=True)]
    ppermute x2, waiting for transfers between devices: 26.3 us -> 18.2 us  [shifted(): lax.ppermute(block, axis, [((i - distance) % count, i) for i in range(cou...]
    all_to_all x2 -> x1, waiting for transfers between devices: 14.7 us -> 8.04 us  [exchanged(): lax.all_to_all(blocks, 'tensor', 0, 0, axis_index_groups=groups, tiled=True)]
    unnamed x7 -> x6, local copies, waits for them, and re-layouts: 2.31 us -> 0.02 us
    pallas_call x1 -> x3, Pallas kernels: 3.51 us -> 5.67 us  [the longest x1 4.05 us: step(): pl.pallas_call(forward_kernel, out_shape=(struct((half, weight.shape[0]))...]
    dot_general x1 -> x2, matrix products: 0.83 us -> 2.87 us  [dot(): lax.dot_general(a, b, (((ca,), (cb,)), ((), ())), preferred_element_type=...]
  transfers between devices with their start and end apart: 4 -> 5, of which waited for: 3 -> 4; matrix products, arithmetic and copies ran while one was open for 1% -> 1% of each run, Pallas kernels for 5% -> 6%
where the time goes in v2:
time: 85.1 us; the launch traced here: 84.6 us
  starting transfers between devices  29.2 us (34%)
  waiting for transfers between devices  27.9 us (33%)
  blocking collectives  12.8 us (15%)
  Pallas kernels  9.87 us (12%)
  matrix products  2.87 us (3%)
  other arithmetic  1.18 us (1%)
    ppermute x2, starting transfers between devices, crossed(): lax.ppermute(block, 'tensor', [(i, i ^ 1) for i in range(lax.axis_size('t...  21.2 us
    ppermute x2, waiting for transfers between devices, shifted(): lax.ppermute(block, axis, [((i - distance) % count, i) for i in range(cou...  18.2 us
    all_to_all x1, blocking collectives, exchanged(): lax.all_to_all(blocks, 'tensor', 0, 0, axis_index_groups=groups, tiled=True)  12.8 us
    all_to_all x1, waiting for transfers between devices, exchanged(): lax.all_to_all(blocks, 'tensor', 0, 0, axis_index_groups=groups, tiled=True)  8.04 us
    all_to_all x1, starting transfers between devices, exchanged(): lax.all_to_all(blocks, 'tensor', 0, 0, axis_index_groups=groups, tiled=True)  4.14 us
    pallas_call x1, Pallas kernels, step(): pl.pallas_call(forward_kernel, out_shape=(struct((half, weight.shape[0]))...  4.05 us
    ppermute x2, starting transfers between devices, shifted(): lax.ppermute(block, axis, [((i - distance) % count, i) for i in range(cou...  3.84 us
    dot_general x2, matrix products, dot(): lax.dot_general(a, b, (((ca,), (cb,)), ((), ())), preferred_element_type=...  2.87 us
  transfers between devices with their start and end apart: 5, of which 4 were waited for; matrix products, arithmetic and copies ran while one was open for 1% of the time, Pallas kernels for 6%

profile of v2, /device:TPU:1, one launch (start us, length us, event | category | flops | bytes accessed | tf_op | source)
XLA Modules:
  0.0 84.6 jit_solution(2004858906460313298)
XLA Ops:
  0.6 0.0 copy-start
  0.6 0.0 copy-start.1
  0.7 4.0 %front.1 = (bf16[64,256]{1,0:T(8,128)(2,1)}, bf16[64,4096]{1,0:T(8,128)(2,1)}) custom-call(bf16[1,3,128,256]{3,2,1,0:T(8,128)(2,1)} %qkv_hbm.1, bf16[1,256,4096]{2,1,0:T(8,128)(2,1)} %weight_hbm.1), custom_call_target="tpu_custom_call" | custom-call | tf_op jit(solution)/shard_map/front/pallas_call | solution.py:135
  4.7 16.0 %collective-permute-start = (bf16[64,4096]{1,0:T(8,128)(2,1)}, bf16[64,4096]{1,0:T(8,128)(2,1)S(1)}, u32[]{:S(2)}, u32[]{:S(2)}) collective-permute-start(bf16[64,4096]{1,0:T(8,128)(2,1)} %get-tuple-element.11), channel_id=1, source_target_pairs={{0,1},{1,0},{2,3},{3,2},{4,5},{5,4},{6,7},{7,6},{8,9},{9,8},{10,11... | collective-permute-start | bytes 1572872 | tf_op jit(solution)/shard_map/ppermute | solution.py:120
  20.7 1.7 %collective-permute-done = bf16[64,4096]{1,0:T(8,128)(2,1)S(1)} collective-permute-done((bf16[64,4096]{1,0:T(8,128)(2,1)}, bf16[64,4096]{1,0:T(8,128)(2,1)S(1)}, u32[]{:S(2)}, u32[]{:S(2)}) %collective-permute-start) | collective-permute-done | bytes 524320 | tf_op jit(solution)/shard_map/ppermute | solution.py:120
  22.5 0.0 copy-done.1
  22.5 2.0 %fusion.8 = bf16[8,8,4096]{2,1,0:T(8,128)(2,1)} fusion(bf16[64,4096]{1,0:T(8,128)(2,1)S(1)} %collective-permute-done, bf16[64,256]{1,0:T(8,128)(2,1)} %get-tuple-element.10, bf16[1,256,4096]{2,1,0:T(8,128)(2,1)S(1)} %copy-done.1), kind=kOutput, calls=%fused_computation.7 | convolution fusion | flops 135004160 | bytes 3178496 | tf_op jit(solution)/shard_map/dot_general | solution.py:26
  24.5 4.1 %all-to-all-start = ((bf16[8,8,4096]{2,1,0:T(8,128)(2,1)}), bf16[8,8,4096]{2,1,0:T(8,128)(2,1)}, u32[]{:S(2)}, u32[]{:S(2)}) async-start(bf16[8,8,4096]{2,1,0:T(8,128)(2,1)} %fusion.8), calls=%async_computation | async-start | bytes 1048576 | tf_op jit(solution)/shard_map/all_to_all | solution.py:126
  28.7 2.5 %pick.1 = (bf16[2,3,128,256]{3,2,1,0:T(8,128)(2,1)}, bf16[8,4096]{1,0:T(8,128)(2,1)}) custom-call(s32[64]{0:T(128)} %slots.1, bf16[1,2,3,128,256]{4,3,2,1,0:T(8,128)(2,1)} %stash.1, bf16[1,3,128,256]{3,2,1,0:T(8,128)(2,1)} %qkv_hbm.1, bf16[1,128,4096]{2,1,0:T(8,128)(2,1)} %residual.1), custom_call_target="tpu_custom_call" | custom-call | tf_op jit(solution)/shard_map/pick/pallas_call | solution.py:153
  31.2 0.0 copy-start.2
  31.2 8.0 %all-to-all-done = bf16[8,8,4096]{2,1,0:T(8,128)(2,1)} async-done(((bf16[8,8,4096]{2,1,0:T(8,128)(2,1)}), bf16[8,8,4096]{2,1,0:T(8,128)(2,1)}, u32[]{:S(2)}, u32[]{:S(2)}) %all-to-all-start) | async-done | bytes 524320 | tf_op jit(solution)/shard_map/all_to_all | solution.py:126
  39.2 1.2 %fusion.9 = bf16[8,4096]{1,0:T(8,128)(2,1)S(1)} fusion(bf16[8,4096]{1,0:T(8,128)(2,1)} %get-tuple-element.9, bf16[8,8,4096]{2,1,0:T(8,128)(2,1)} %all-to-all-done), kind=kLoop, calls=%fused_computation.9 | loop fusion | flops 589824 | bytes 655360 | tf_op jit(solution)/shard_map/convert_element_type | solution.py:166
  40.4 1.9 %collective-permute-start.1 = (bf16[8,4096]{1,0:T(8,128)(2,1)S(1)}, bf16[8,4096]{1,0:T(8,128)(2,1)S(1)}, u32[]{:S(2)}, u32[]{:S(2)}) collective-permute-start(bf16[8,4096]{1,0:T(8,128)(2,1)S(1)} %fusion.9), channel_id=1, source_target_pairs={{1008,0},{0,16},{16,32},{32,48},{48,64},{64,80},{80,96},{96,112},{... | collective-permute-start | bytes 196616 | tf_op jit(solution)/shard_map/ppermute | solution.py:116
  42.3 8.4 %collective-permute-done.1 = bf16[8,4096]{1,0:T(8,128)(2,1)S(1)} collective-permute-done((bf16[8,4096]{1,0:T(8,128)(2,1)S(1)}, bf16[8,4096]{1,0:T(8,128)(2,1)S(1)}, u32[]{:S(2)}, u32[]{:S(2)}) %collective-permute-start.1) | collective-permute-done | bytes 65568 | tf_op jit(solution)/shard_map/ppermute | solution.py:116
  50.7 12.8 %all_to_all.10 = bf16[8,8,4096]{2,1,0:T(8,128)(2,1)S(1)} all-to-all(bf16[8,8,4096]{2,1,0:T(8,128)(2,1)S(1)} %broadcast_in_dim.2), channel_id=1, replica_groups={{0,2,4,6,8,10,12,14},{1,3,5,7,9,11,13,15},{16,18,20,22,24,26,28,30},{17..., dimensions={0} | all-to-all | bytes 1048576 | tf_op jit(solution)/shard_map/all_to_all | solution.py:126
  63.6 5.2 %collective-permute-start.2 = (bf16[64,4096]{1,0:T(8,128)(2,1)S(1)}, bf16[64,4096]{1,0:T(8,128)(2,1)S(1)}, u32[]{:S(2)}, u32[]{:S(2)}) collective-permute-start(bf16[64,4096]{1,0:T(8,128)(2,1)S(1)} %bitcast.56), channel_id=1, source_target_pairs={{0,1},{1,0},{2,3},{3,2},{4,5},{5,4},{6,7},{7,6},{8,9},{9,8},{10,11... | collective-permute-start | bytes 1572872 | tf_op jit(solution)/shard_map/ppermute | solution.py:120
  68.7 0.0 copy-done.2
  68.7 1.9 %collective-permute-start.3 = (bf16[2,3,128,256]{3,2,1,0:T(8,128)(2,1)S(1)}, bf16[2,3,128,256]{3,2,1,0:T(8,128)(2,1)S(1)}, u32[]{:S(2)}, u32[]{:S(2)}) collective-permute-start(bf16[2,3,128,256]{3,2,1,0:T(8,128)(2,1)S(1)} %copy-done.2), channel_id=1, source_target_pairs={{512,0},{528,16},{544,32},{560,48},{576,64},{592,80},{608,96},{624... | collective-permute-start | bytes 1179656 | tf_op jit(solution)/shard_map/ppermute | solution.py:116
  70.7 0.0 copy-done
  70.7 0.8 fusion.4.grad_context
  71.5 9.8 %collective-permute-done.3.pair = bf16[2,3,128,256]{3,2,1,0:T(8,128)(2,1)S(1)} collective-permute-done((bf16[2,3,128,256]{3,2,1,0:T(8,128)(2,1)S(1)}, bf16[2,3,128,256]{3,2,1,0:T(8,128)(2,1)S(1)}, u32[]{:S(2)}, u32[]{:S(2)}) %collective-permute-start.3) | collective-permute-done | bytes 393248 | tf_op jit(solution)/shard_map/ppermute | solution.py:116
  81.3 1.7 %back.1 = (bf16[1,3,128,256]{3,2,1,0:T(8,128)(2,1)}, bf16[1,3,128,256]{3,2,1,0:T(8,128)(2,1)}) custom-call(bf16[2,3,128,256]{3,2,1,0:T(8,128)(2,1)S(1)} %collective-permute-done.3.pair, bf16[128,256]{1,0:T(8,128)(2,1)S(1)} %fusion.4.grad_context), custom_call_target="tpu_custom_call" | custom-call | tf_op jit(solution)/shard_map/back/pallas_call | solution.py:170
  83.0 0.8 place.1.refs_0_
  83.8 0.0 collective-permute-done.2.block
  83.8 0.8 join.1
  (1 shorter events, 0.0 us)
Async XLA Ops:
  0.6 70.0 %copy-start = (bf16[1,128,4096]{2,1,0:T(8,128)(2,1)S(1)}, bf16[1,128,4096]{2,1,0:T(8,128)(2,1)}, u32[]{:S(2)}) copy-start(bf16[1,128,4096]{2,1,0:T(8,128)(2,1)} %param.10) | copy-start | bytes 3145732
  0.6 21.8 %copy-start.1 = (bf16[1,256,4096]{2,1,0:T(8,128)(2,1)S(1)}, bf16[1,256,4096]{2,1,0:T(8,128)(2,1)}, u32[]{:S(2)}) copy-start(bf16[1,256,4096]{2,1,0:T(8,128)(2,1)} %weight_hbm.1) | copy-start | bytes 6291460
  4.7 17.8 %collective-permute-start = (bf16[64,4096]{1,0:T(8,128)(2,1)}, bf16[64,4096]{1,0:T(8,128)(2,1)S(1)}, u32[]{:S(2)}, u32[]{:S(2)}) collective-permute-start(bf16[64,4096]{1,0:T(8,128)(2,1)} %get-tuple-element.11), channel_id=1, source_target_pairs={{0,1},{1,0},{2,3},{3,2},{4,5},{5,4},{6,7},{7,6},{8,9},{9,8},{10,11... | collective-permute-start | bytes 1572872 | tf_op jit(solution)/shard_map/ppermute | solution.py:120
  24.5 14.7 %all-to-all-start = ((bf16[8,8,4096]{2,1,0:T(8,128)(2,1)}), bf16[8,8,4096]{2,1,0:T(8,128)(2,1)}, u32[]{:S(2)}, u32[]{:S(2)}) async-start(bf16[8,8,4096]{2,1,0:T(8,128)(2,1)} %fusion.8), calls=%async_computation | async-start | bytes 1048576 | tf_op jit(solution)/shard_map/all_to_all | solution.py:126
  31.2 37.6 %copy-start.2 = (bf16[2,3,128,256]{3,2,1,0:T(8,128)(2,1)S(1)}, bf16[2,3,128,256]{3,2,1,0:T(8,128)(2,1)}, u32[]{:S(2)}) copy-start(bf16[2,3,128,256]{3,2,1,0:T(8,128)(2,1)} %get-tuple-element.12) | copy-start | bytes 1179652
  40.4 10.3 %collective-permute-start.1 = (bf16[8,4096]{1,0:T(8,128)(2,1)S(1)}, bf16[8,4096]{1,0:T(8,128)(2,1)S(1)}, u32[]{:S(2)}, u32[]{:S(2)}) collective-permute-start(bf16[8,4096]{1,0:T(8,128)(2,1)S(1)} %fusion.9), channel_id=1, source_target_pairs={{1008,0},{0,16},{16,32},{32,48},{48,64},{64,80},{80,96},{96,112},{... | collective-permute-start | bytes 196616 | tf_op jit(solution)/shard_map/ppermute | solution.py:116
  63.6 20.3 %collective-permute-start.2 = (bf16[64,4096]{1,0:T(8,128)(2,1)S(1)}, bf16[64,4096]{1,0:T(8,128)(2,1)S(1)}, u32[]{:S(2)}, u32[]{:S(2)}) collective-permute-start(bf16[64,4096]{1,0:T(8,128)(2,1)S(1)} %bitcast.56), channel_id=1, source_target_pairs={{0,1},{1,0},{2,3},{3,2},{4,5},{5,4},{6,7},{7,6},{8,9},{9,8},{10,11... | collective-permute-start | bytes 1572872 | tf_op jit(solution)/shard_map/ppermute | solution.py:120
  68.7 12.6 %collective-permute-start.3 = (bf16[2,3,128,256]{3,2,1,0:T(8,128)(2,1)S(1)}, bf16[2,3,128,256]{3,2,1,0:T(8,128)(2,1)S(1)}, u32[]{:S(2)}, u32[]{:S(2)}) collective-permute-start(bf16[2,3,128,256]{3,2,1,0:T(8,128)(2,1)S(1)} %copy-done.2), channel_id=1, source_target_pairs={{512,0},{528,16},{544,32},{560,48},{576,64},{592,80},{608,96},{624... | collective-permute-start | bytes 1179656 | tf_op jit(solution)/shard_map/ppermute | solution.py:116

commit v3 on v2

--- a/solution.py
+++ b/solution.py
@@ -40,15 +40,14 @@
     return weights / jnp.sum(weights, axis=1, keepdims=True)
 
 
-def forward_kernel(qkv_hbm, weight_hbm, own_context, out_hbm, qkv, weight, context, out, sems):
-    tiles, tile = weight.shape[0], weight.shape[2]
-    half = own_context.shape[0]
+def forward_kernel(qkv_hbm, weight_hbm, own_hbm, theirs_hbm, qkv, weight, context, own, theirs, sems):
+    half, width = theirs.shape
+    depth = weight.shape[0] // 2
     load_qkv = pltpu.make_async_copy(qkv_hbm.at[0], qkv, sems.at[0])
-    loads, stores = [], []
-    for n in range(tiles):
-        c = slice(n * tile, (n + 1) * tile)
-        loads.append(pltpu.make_async_copy(weight_hbm.at[0, :, c], weight.at[n], sems.at[1 + n]))
-        stores.append(pltpu.make_async_copy(out.at[n], out_hbm.at[:, c], sems.at[1 + tiles + n]))
+    loads = [
+        pltpu.make_async_copy(weight_hbm.at[0, part], weight.at[part], sems.at[1 + k])
+        for k, part in enumerate((slice(0, depth), slice(depth, 2 * depth)))
+    ]
     load_qkv.start()
     for load in loads:
         load.start()
@@ -58,17 +57,26 @@
         probs = probs_of(qkv[0, :, c], qkv[1, :, c]).astype(BF)
         context[:, c] = dot(probs, qkv[2, :, c], 1, 0).astype(BF)
     core = core_of_chip()
-    own_context[...] = context[pl.ds(pl.multiple_of(core * half, half), half), :]
-    theirs = context[pl.ds(pl.multiple_of((1 - core) * half, half), half), :]
-    for n in range(tiles):
-        loads[n].wait()
-        out[n] = dot(theirs, weight[n], 1, 0).astype(BF)
-        stores[n].start()
+    first = pl.multiple_of((1 - core) * half, half)
+    second = pl.multiple_of(core * half, half)
+    both = jnp.concatenate([context[pl.ds(first, half), :], context[pl.ds(second, half), :]], axis=0)
+    for load in loads:
+        load.wait()
+    stores = []
+    for n, c in enumerate((slice(0, width // 2), slice(width // 2, width))):
+        product = dot(both, weight[:, c], 1, 0)
+        theirs[:, c] = product[:half].astype(BF)
+        own[:, c] = product[half:]
+        for k, (near, far) in enumerate(((theirs, theirs_hbm), (own, own_hbm))):
+            stores.append(pltpu.make_async_copy(near.at[:, c], far.at[:, c], sems.at[3 + 2 * n + k]))
+            stores[-1].start()
     for store in stores:
         store.wait()
 
 
-def pick_kernel(slots, stash, qkv, residual, pair, rows, sems):
+def aside_kernel(
+    slots, stash, qkv, residual, grad_hbm, weight_hbm, pair, rows, grad_context, grad, weight, sems
+):
     sections = lax.axis_size("pipe")
     partner = lax.rem(lax.axis_index("pipe") + sections // 2, sections)
     share = rows.shape[0]
@@ -76,14 +84,17 @@
     first = core_of_chip() * half + lax.div(lax.axis_index("tensor"), 2) * share
     first = pl.multiple_of(first, share)
     copies = (
-        pltpu.make_async_copy(stash.at[0, slots[partner]], pair.at[0], sems.at[0]),
-        pltpu.make_async_copy(qkv.at[0], pair.at[1], sems.at[1]),
-        pltpu.make_async_copy(residual.at[0, pl.ds(first, share)], rows, sems.at[2]),
+        pltpu.make_async_copy(grad_hbm.at[0], grad, sems.at[0]),
+        pltpu.make_async_copy(weight_hbm.at[0], weight, sems.at[1]),
+        pltpu.make_async_copy(stash.at[0, slots[partner]], pair.at[0], sems.at[2]),
+        pltpu.make_async_copy(qkv.at[0], pair.at[1], sems.at[3]),
+        pltpu.make_async_copy(residual.at[0, pl.ds(first, share)], rows, sems.at[4]),
     )
     for copy in copies:
         copy.start()
     for copy in copies:
         copy.wait()
+    grad_context[...] = dot(grad[...], weight[...], 1, 1).astype(BF)
 
 
 def place_kernel(other, block, *refs):
@@ -128,38 +139,43 @@
 
 def step(residual, out_proj, attn_in, stash_slots, grad_in, stash_slot):
     sections, members = lax.axis_size("pipe"), lax.axis_size("tensor")
-    weight = out_proj[0]
     rows, width = residual.shape[1:]
     chips, half, share = members // 2, rows // 2, rows // members
-    tiles = 4
-    own_context, product = pl.pallas_call(
+    own, theirs = pl.pallas_call(
         forward_kernel,
-        out_shape=(struct((half, weight.shape[0])), struct((half, width))),
+        out_shape=(struct((half, width), F32), struct((half, width))),
         in_specs=[ANY, ANY],
-        out_specs=(VMEM, ANY),
+        out_specs=(ANY, ANY),
         scratch_shapes=[
             pltpu.VMEM(attn_in.shape[1:], BF),
-            pltpu.VMEM((tiles, weight.shape[0], width // tiles), BF),
-            pltpu.VMEM((rows, weight.shape[0]), BF),
-            pltpu.VMEM((tiles, half, width // tiles), BF),
-            pltpu.SemaphoreType.DMA((1 + 2 * tiles,)),
+            pltpu.VMEM(out_proj.shape[1:], BF),
+            pltpu.VMEM((rows, out_proj.shape[1]), BF),
+            pltpu.VMEM((half, width), F32),
+            pltpu.VMEM((half, width), BF),
+            pltpu.SemaphoreType.DMA((7,)),
         ],
         name="front",
     )(attn_in, out_proj)
-    received = crossed(product)
-    own = dot(own_context, weight, 1, 0)
+    received = crossed(theirs)
     partial = (own + received.astype(F32)).astype(BF).reshape(chips, share, width)
     parts = exchanged(partial)
-    pair, own_rows = pl.pallas_call(
-        pick_kernel,
-        out_shape=(struct((2, *attn_in.shape[1:])), struct((share, width))),
-        in_specs=[SMEM, ANY, ANY, ANY],
-        out_specs=(VMEM, VMEM),
-        scratch_shapes=[pltpu.SemaphoreType.DMA((3,))],
-        name="pick",
-    )(stash_slot, stash_slots, attn_in, residual)
+    pair, own_rows, grad_context = pl.pallas_call(
+        aside_kernel,
+        out_shape=(
+            struct((2, *attn_in.shape[1:])),
+            struct((share, width)),
+            struct((rows, out_proj.shape[1])),
+        ),
+        in_specs=[SMEM, ANY, ANY, ANY, ANY, ANY],
+        out_specs=(VMEM, VMEM, VMEM),
+        scratch_shapes=[
+            pltpu.VMEM(grad_in.shape[1:], BF),
+            pltpu.VMEM(out_proj.shape[1:], BF),
+            pltpu.SemaphoreType.DMA((5,)),
+        ],
+        name="aside",
+    )(stash_slot, stash_slots, attn_in, residual, grad_in, out_proj)
     swapped = shifted(pair, "pipe", sections // 2)
-    grad_context = dot(grad_in[0], weight, 1, 1).astype(BF)
     total = own_rows.astype(F32)
     for chip in range(chips):
         total = total + parts[chip].astype(F32)

time: 85.1 us -> 83.9 us (0.986)
  matrix products: 2.87 us -> 0 us
  other arithmetic: 1.18 us -> 3.03 us
    dot_general x2 -> x0, matrix products: 2.87 us -> none  [dot(): lax.dot_general(a, b, (((ca,), (cb,)), ((), ())), preferred_element_type=...]
    reshape x0 -> x1, other arithmetic: none -> 2.11 us  [step(): (own + received.astype(F32)).astype(BF).reshape(chips, share, width)]
    all_to_all x1, waiting for transfers between devices: 8.04 us -> 6.34 us  [exchanged(): lax.all_to_all(blocks, 'tensor', 0, 0, axis_index_groups=groups, tiled=True)]
    ppermute x2, waiting for transfers between devices: 18.2 us -> 19.6 us  [shifted(): lax.ppermute(block, axis, [((i - distance) % count, i) for i in range(cou...]
  transfers between devices with their start and end apart: 5 -> 5, of which waited for: 4 -> 4; matrix products, arithmetic and copies ran while one was open for 1% -> 0% of each run, Pallas kernels for 6% -> 8%
where the time goes in v3:
time: 83.9 us; the launch traced here: 83.5 us
  starting transfers between devices  28.5 us (34%)
  waiting for transfers between devices  27.7 us (33%)
  blocking collectives  12.8 us (15%)
  Pallas kernels  10.6 us (13%)
  other arithmetic  3.03 us (4%)
    ppermute x2, starting transfers between devices, crossed(): lax.ppermute(block, 'tensor', [(i, i ^ 1) for i in range(lax.axis_size('t...  21.2 us
    ppermute x2, waiting for transfers between devices, shifted(): lax.ppermute(block, axis, [((i - distance) % count, i) for i in range(cou...  19.6 us
    all_to_all x1, blocking collectives, exchanged(): lax.all_to_all(blocks, 'tensor', 0, 0, axis_index_groups=groups, tiled=True)  12.8 us
    all_to_all x1, waiting for transfers between devices, exchanged(): lax.all_to_all(blocks, 'tensor', 0, 0, axis_index_groups=groups, tiled=True)  6.34 us
    pallas_call x1, Pallas kernels, step(): pl.pallas_call(aside_kernel, out_shape=(struct((2, *attn_in.shape[1:])),...  4.1 us
    ppermute x2, starting transfers between devices, shifted(): lax.ppermute(block, axis, [((i - distance) % count, i) for i in range(cou...  3.84 us
    all_to_all x1, starting transfers between devices, exchanged(): lax.all_to_all(blocks, 'tensor', 0, 0, axis_index_groups=groups, tiled=True)  3.49 us
    pallas_call x1, Pallas kernels, step(): pl.pallas_call(forward_kernel, out_shape=(struct((half, width), F32), str...  3.2 us
  transfers between devices with their start and end apart: 5, of which 4 were waited for; matrix products, arithmetic and copies ran while one was open for 0% of the time, Pallas kernels for 8%

profile of v3, /device:TPU:1, one launch (start us, length us, event | category | flops | bytes accessed | tf_op | source)
XLA Modules:
  0.0 83.5 jit_solution(17499894484096014307)
XLA Ops:
  0.6 3.2 %front.1 = (f32[64,4096]{1,0:T(8,128)}, bf16[64,4096]{1,0:T(8,128)(2,1)}) custom-call(bf16[1,3,128,256]{3,2,1,0:T(8,128)(2,1)} %qkv_hbm.1, bf16[1,256,4096]{2,1,0:T(8,128)(2,1)} %weight_hbm.3), custom_call_target="tpu_custom_call" | custom-call | tf_op jit(solution)/shard_map/front/pallas_call | solution.py:144
  3.8 16.0 %collective-permute-start = (bf16[64,4096]{1,0:T(8,128)(2,1)}, bf16[64,4096]{1,0:T(8,128)(2,1)S(1)}, u32[]{:S(2)}, u32[]{:S(2)}) collective-permute-start(bf16[64,4096]{1,0:T(8,128)(2,1)} %get-tuple-element.12), channel_id=1, source_target_pairs={{0,1},{1,0},{2,3},{3,2},{4,5},{5,4},{6,7},{7,6},{8,9},{9,8},{10,11... | collective-permute-start | bytes 1572872 | tf_op jit(solution)/shard_map/ppermute | solution.py:131
  19.9 1.7 %collective-permute-done = bf16[64,4096]{1,0:T(8,128)(2,1)S(1)} collective-permute-done((bf16[64,4096]{1,0:T(8,128)(2,1)}, bf16[64,4096]{1,0:T(8,128)(2,1)S(1)}, u32[]{:S(2)}, u32[]{:S(2)}) %collective-permute-start) | collective-permute-done | bytes 524320 | tf_op jit(solution)/shard_map/ppermute | solution.py:131
  21.6 2.1 %fusion = bf16[8,8,4096]{2,1,0:T(8,128)(2,1)} fusion(f32[64,4096]{1,0:T(8,128)} %get-tuple-element.11, bf16[64,4096]{1,0:T(8,128)(2,1)S(1)} %collective-permute-done), kind=kLoop, calls=%fused_computation.1 | loop fusion | flops 786432 | bytes 2097152 | tf_op jit(solution)/shard_map/reshape | solution.py:160
  23.7 3.5 %all-to-all-start = ((bf16[8,8,4096]{2,1,0:T(8,128)(2,1)}), bf16[8,8,4096]{2,1,0:T(8,128)(2,1)S(1)}, u32[]{:S(2)}, u32[]{:S(2)}) async-start(bf16[8,8,4096]{2,1,0:T(8,128)(2,1)} %fusion), calls=%async_computation | async-start | bytes 1048576 | tf_op jit(solution)/shard_map/all_to_all | solution.py:137
  27.2 4.1 %aside.1 = (bf16[2,3,128,256]{3,2,1,0:T(8,128)(2,1)}, bf16[8,4096]{1,0:T(8,128)(2,1)}, bf16[128,256]{1,0:T(8,128)(2,1)}) custom-call(s32[64]{0:T(128)} %slots.1, bf16[1,2,3,128,256]{4,3,2,1,0:T(8,128)(2,1)} %stash.1, bf16[1,3,128,256]{3,2,1,0:T(8,128)(2,1)} %qkv_hbm.1, bf16[1,128,4096]{2,1,0:T(8,128)(2,1)} %residual.1, bf16[1,128,4096]{2,1,0:T(8,128)(2,1)} %grad_hbm.1, ...), custom_call_target="tpu_custom_call" | custom-call | tf_op jit(solution)/shard_map/aside/pallas_call | solution.py:162
  31.3 0.0 copy-start.1
  31.3 0.0 copy-start
  31.3 6.3 %all-to-all-done = bf16[8,8,4096]{2,1,0:T(8,128)(2,1)S(1)} async-done(((bf16[8,8,4096]{2,1,0:T(8,128)(2,1)}), bf16[8,8,4096]{2,1,0:T(8,128)(2,1)S(1)}, u32[]{:S(2)}, u32[]{:S(2)}) %all-to-all-start) | async-done | bytes 524320 | tf_op jit(solution)/shard_map/all_to_all | solution.py:137
  37.7 0.9 %fusion.1 = bf16[8,4096]{1,0:T(8,128)(2,1)S(1)} fusion(bf16[8,4096]{1,0:T(8,128)(2,1)} %get-tuple-element.10, bf16[8,8,4096]{2,1,0:T(8,128)(2,1)S(1)} %all-to-all-done), kind=kLoop, calls=%fused_computation.3 | loop fusion | flops 589824 | bytes 655360 | tf_op jit(solution)/shard_map/convert_element_type | solution.py:182
  38.6 1.9 %collective-permute-start.1 = (bf16[8,4096]{1,0:T(8,128)(2,1)S(1)}, bf16[8,4096]{1,0:T(8,128)(2,1)S(1)}, u32[]{:S(2)}, u32[]{:S(2)}) collective-permute-start(bf16[8,4096]{1,0:T(8,128)(2,1)S(1)} %fusion.1), channel_id=1, source_target_pairs={{1008,0},{0,16},{16,32},{32,48},{48,64},{64,80},{80,96},{96,112},{... | collective-permute-start | bytes 196616 | tf_op jit(solution)/shard_map/ppermute | solution.py:127
  40.5 9.0 %collective-permute-done.1 = bf16[8,4096]{1,0:T(8,128)(2,1)S(1)} collective-permute-done((bf16[8,4096]{1,0:T(8,128)(2,1)S(1)}, bf16[8,4096]{1,0:T(8,128)(2,1)S(1)}, u32[]{:S(2)}, u32[]{:S(2)}) %collective-permute-start.1) | collective-permute-done | bytes 65568 | tf_op jit(solution)/shard_map/ppermute | solution.py:127
  49.6 12.8 %all_to_all.10 = bf16[8,8,4096]{2,1,0:T(8,128)(2,1)S(1)} all-to-all(bf16[8,8,4096]{2,1,0:T(8,128)(2,1)S(1)} %broadcast_in_dim.2), channel_id=1, replica_groups={{0,2,4,6,8,10,12,14},{1,3,5,7,9,11,13,15},{16,18,20,22,24,26,28,30},{17..., dimensions={0} | all-to-all | bytes 1048576 | tf_op jit(solution)/shard_map/all_to_all | solution.py:137
  62.4 5.2 %collective-permute-start.2 = (bf16[64,4096]{1,0:T(8,128)(2,1)S(1)}, bf16[64,4096]{1,0:T(8,128)(2,1)S(1)}, u32[]{:S(2)}, u32[]{:S(2)}) collective-permute-start(bf16[64,4096]{1,0:T(8,128)(2,1)S(1)} %bitcast.43), channel_id=1, source_target_pairs={{0,1},{1,0},{2,3},{3,2},{4,5},{5,4},{6,7},{7,6},{8,9},{9,8},{10,11... | collective-permute-start | bytes 1572872 | tf_op jit(solution)/shard_map/ppermute | solution.py:131
  67.6 0.0 copy-done.1
  67.6 1.9 %collective-permute-start.3 = (bf16[2,3,128,256]{3,2,1,0:T(8,128)(2,1)S(1)}, bf16[2,3,128,256]{3,2,1,0:T(8,128)(2,1)S(1)}, u32[]{:S(2)}, u32[]{:S(2)}) collective-permute-start(bf16[2,3,128,256]{3,2,1,0:T(8,128)(2,1)S(1)} %copy-done.1), channel_id=1, source_target_pairs={{512,0},{528,16},{544,32},{560,48},{576,64},{592,80},{608,96},{624... | collective-permute-start | bytes 1179656 | tf_op jit(solution)/shard_map/ppermute | solution.py:127
  69.5 10.6 %collective-permute-done.3.pair = bf16[2,3,128,256]{3,2,1,0:T(8,128)(2,1)S(1)} collective-permute-done((bf16[2,3,128,256]{3,2,1,0:T(8,128)(2,1)S(1)}, bf16[2,3,128,256]{3,2,1,0:T(8,128)(2,1)S(1)}, u32[]{:S(2)}, u32[]{:S(2)}) %collective-permute-start.3) | collective-permute-done | bytes 393248 | tf_op jit(solution)/shard_map/ppermute | solution.py:127
  80.1 0.0 copy-done
  80.1 1.7 %back.1 = (bf16[1,3,128,256]{3,2,1,0:T(8,128)(2,1)}, bf16[1,3,128,256]{3,2,1,0:T(8,128)(2,1)}) custom-call(bf16[2,3,128,256]{3,2,1,0:T(8,128)(2,1)S(1)} %collective-permute-done.3.pair, bf16[128,256]{1,0:T(8,128)(2,1)S(1)} %copy-done), custom_call_target="tpu_custom_call" | custom-call | tf_op jit(solution)/shard_map/back/pallas_call | solution.py:186
  81.8 0.8 place.1.refs_0_
  82.7 0.0 collective-permute-done.2.block
  82.7 0.8 join.1
  (1 shorter events, 0.0 us)
Async XLA Ops:
  3.8 17.8 %collective-permute-start = (bf16[64,4096]{1,0:T(8,128)(2,1)}, bf16[64,4096]{1,0:T(8,128)(2,1)S(1)}, u32[]{:S(2)}, u32[]{:S(2)}) collective-permute-start(bf16[64,4096]{1,0:T(8,128)(2,1)} %get-tuple-element.12), channel_id=1, source_target_pairs={{0,1},{1,0},{2,3},{3,2},{4,5},{5,4},{6,7},{7,6},{8,9},{9,8},{10,11... | collective-permute-start | bytes 1572872 | tf_op jit(solution)/shard_map/ppermute | solution.py:131
  23.7 14.0 %all-to-all-start = ((bf16[8,8,4096]{2,1,0:T(8,128)(2,1)}), bf16[8,8,4096]{2,1,0:T(8,128)(2,1)S(1)}, u32[]{:S(2)}, u32[]{:S(2)}) async-start(bf16[8,8,4096]{2,1,0:T(8,128)(2,1)} %fusion), calls=%async_computation | async-start | bytes 1048576 | tf_op jit(solution)/shard_map/all_to_all | solution.py:137
  31.3 36.3 %copy-start.1 = (bf16[2,3,128,256]{3,2,1,0:T(8,128)(2,1)S(1)}, bf16[2,3,128,256]{3,2,1,0:T(8,128)(2,1)}, u32[]{:S(2)}) copy-start(bf16[2,3,128,256]{3,2,1,0:T(8,128)(2,1)} %get-tuple-element.13) | copy-start | bytes 1179652
  31.3 48.8 %copy-start = (bf16[128,256]{1,0:T(8,128)(2,1)S(1)}, bf16[128,256]{1,0:T(8,128)(2,1)}, u32[]{:S(2)}) copy-start(bf16[128,256]{1,0:T(8,128)(2,1)} %get-tuple-element.14.grad_context) | copy-start | bytes 196612
  38.6 10.9 %collective-permute-start.1 = (bf16[8,4096]{1,0:T(8,128)(2,1)S(1)}, bf16[8,4096]{1,0:T(8,128)(2,1)S(1)}, u32[]{:S(2)}, u32[]{:S(2)}) collective-permute-start(bf16[8,4096]{1,0:T(8,128)(2,1)S(1)} %fusion.1), channel_id=1, source_target_pairs={{1008,0},{0,16},{16,32},{32,48},{48,64},{64,80},{80,96},{96,112},{... | collective-permute-start | bytes 196616 | tf_op jit(solution)/shard_map/ppermute | solution.py:127
  62.4 20.3 %collective-permute-start.2 = (bf16[64,4096]{1,0:T(8,128)(2,1)S(1)}, bf16[64,4096]{1,0:T(8,128)(2,1)S(1)}, u32[]{:S(2)}, u32[]{:S(2)}) collective-permute-start(bf16[64,4096]{1,0:T(8,128)(2,1)S(1)} %bitcast.43), channel_id=1, source_target_pairs={{0,1},{1,0},{2,3},{3,2},{4,5},{5,4},{6,7},{7,6},{8,9},{9,8},{10,11... | collective-permute-start | bytes 1572872 | tf_op jit(solution)/shard_map/ppermute | solution.py:131
  67.6 12.6 %collective-permute-start.3 = (bf16[2,3,128,256]{3,2,1,0:T(8,128)(2,1)S(1)}, bf16[2,3,128,256]{3,2,1,0:T(8,128)(2,1)S(1)}, u32[]{:S(2)}, u32[]{:S(2)}) collective-permute-start(bf16[2,3,128,256]{3,2,1,0:T(8,128)(2,1)S(1)} %copy-done.1), channel_id=1, source_target_pairs={{512,0},{528,16},{544,32},{560,48},{576,64},{592,80},{608,96},{624... | collective-permute-start | bytes 1179656 | tf_op jit(solution)/shard_map/ppermute | solution.py:127

commit v4 on v3

--- a/solution.py
+++ b/solution.py
@@ -15,6 +15,7 @@
 VMEM = pl.BlockSpec(memory_space=pltpu.VMEM)
 SMEM = pl.BlockSpec(memory_space=pltpu.SMEM)
 ANY = pl.BlockSpec(memory_space=pl.ANY)
+HBM = pl.BlockSpec(memory_space=pltpu.HBM)
 SMALL = pltpu.CompilerParams(vmem_limit_bytes=4 << 20)
 
 
@@ -40,7 +41,7 @@
     return weights / jnp.sum(weights, axis=1, keepdims=True)
 
 
-def forward_kernel(qkv_hbm, weight_hbm, own_hbm, theirs_hbm, qkv, weight, context, own, theirs, sems):
+def forward_kernel(qkv_hbm, weight_hbm, own, theirs_hbm, qkv, weight, context, theirs, sems):
     half, width = theirs.shape
     depth = weight.shape[0] // 2
     load_qkv = pltpu.make_async_copy(qkv_hbm.at[0], qkv, sems.at[0])
@@ -67,16 +68,13 @@
         product = dot(both, weight[:, c], 1, 0)
         theirs[:, c] = product[:half].astype(BF)
         own[:, c] = product[half:]
-        for k, (near, far) in enumerate(((theirs, theirs_hbm), (own, own_hbm))):
-            stores.append(pltpu.make_async_copy(near.at[:, c], far.at[:, c], sems.at[3 + 2 * n + k]))
-            stores[-1].start()
+        stores.append(pltpu.make_async_copy(theirs.at[:, c], theirs_hbm.at[:, c], sems.at[3 + n]))
+        stores[-1].start()
     for store in stores:
         store.wait()
 
 
-def aside_kernel(
-    slots, stash, qkv, residual, grad_hbm, weight_hbm, pair, rows, grad_context, grad, weight, sems
-):
+def pick_kernel(slots, stash, qkv, residual, pair, rows, sems):
     sections = lax.axis_size("pipe")
     partner = lax.rem(lax.axis_index("pipe") + sections // 2, sections)
     share = rows.shape[0]
@@ -84,17 +82,26 @@
     first = core_of_chip() * half + lax.div(lax.axis_index("tensor"), 2) * share
     first = pl.multiple_of(first, share)
     copies = (
+        pltpu.make_async_copy(stash.at[0, slots[partner]], pair.at[0], sems.at[0]),
+        pltpu.make_async_copy(qkv.at[0], pair.at[1], sems.at[1]),
+        pltpu.make_async_copy(residual.at[0, pl.ds(first, share)], rows, sems.at[2]),
+    )
+    for copy in copies:
+        copy.start()
+    for copy in copies:
+        copy.wait()
+
+
+def grad_kernel(grad_hbm, weight_hbm, out, grad, weight, sems):
+    copies = (
         pltpu.make_async_copy(grad_hbm.at[0], grad, sems.at[0]),
         pltpu.make_async_copy(weight_hbm.at[0], weight, sems.at[1]),
-        pltpu.make_async_copy(stash.at[0, slots[partner]], pair.at[0], sems.at[2]),
-        pltpu.make_async_copy(qkv.at[0], pair.at[1], sems.at[3]),
-        pltpu.make_async_copy(residual.at[0, pl.ds(first, share)], rows, sems.at[4]),
     )
     for copy in copies:
         copy.start()
     for copy in copies:
         copy.wait()
-    grad_context[...] = dot(grad[...], weight[...], 1, 1).astype(BF)
+    out[...] = dot(grad[...], weight[...], 1, 1).astype(BF)
 
 
 def place_kernel(other, block, *refs):
@@ -144,38 +151,43 @@
     own, theirs = pl.pallas_call(
         forward_kernel,
         out_shape=(struct((half, width), F32), struct((half, width))),
-        in_specs=[ANY, ANY],
-        out_specs=(ANY, ANY),
+        in_specs=[HBM, HBM],
+        out_specs=(VMEM, HBM),
         scratch_shapes=[
             pltpu.VMEM(attn_in.shape[1:], BF),
             pltpu.VMEM(out_proj.shape[1:], BF),
             pltpu.VMEM((rows, out_proj.shape[1]), BF),
-            pltpu.VMEM((half, width), F32),
             pltpu.VMEM((half, width), BF),
-            pltpu.SemaphoreType.DMA((7,)),
+            pltpu.SemaphoreType.DMA((5,)),
         ],
+        compiler_params=pltpu.CompilerParams(vmem_limit_bytes=52 << 20),
         name="front",
     )(attn_in, out_proj)
     received = crossed(theirs)
-    partial = (own + received.astype(F32)).astype(BF).reshape(chips, share, width)
+    partial = (own + received.astype(F32)).astype(BF)
+    partial = partial.reshape(chips, share, width)
     parts = exchanged(partial)
-    pair, own_rows, grad_context = pl.pallas_call(
-        aside_kernel,
-        out_shape=(
-            struct((2, *attn_in.shape[1:])),
-            struct((share, width)),
-            struct((rows, out_proj.shape[1])),
-        ),
-        in_specs=[SMEM, ANY, ANY, ANY, ANY, ANY],
-        out_specs=(VMEM, VMEM, VMEM),
+    pair, own_rows = pl.pallas_call(
+        pick_kernel,
+        out_shape=(struct((2, *attn_in.shape[1:])), struct((share, width))),
+        in_specs=[SMEM, HBM, HBM, HBM],
+        out_specs=(VMEM, VMEM),
+        scratch_shapes=[pltpu.SemaphoreType.DMA((3,))],
+        name="pick",
+    )(stash_slot, stash_slots, attn_in, residual)
+    swapped = shifted(pair, "pipe", sections // 2)
+    grad_context = pl.pallas_call(
+        grad_kernel,
+        out_shape=struct((rows, out_proj.shape[1])),
+        in_specs=[HBM, HBM],
+        out_specs=VMEM,
         scratch_shapes=[
             pltpu.VMEM(grad_in.shape[1:], BF),
             pltpu.VMEM(out_proj.shape[1:], BF),
-            pltpu.SemaphoreType.DMA((5,)),
+            pltpu.SemaphoreType.DMA((2,)),
         ],
-        name="aside",
-    )(stash_slot, stash_slots, attn_in, residual, grad_in, out_proj)
-    swapped = shifted(pair, "pipe", sections // 2)
+        name="gctx",
+    )(grad_in, out_proj)
     total = own_rows.astype(F32)
     for chip in range(chips):
         total = total + parts[chip].astype(F32)
@@ -195,8 +207,8 @@
     placed = pl.pallas_call(
         functools.partial(place_kernel, False),
         out_shape=struct(residual.shape),
-        in_specs=[VMEM],
-        out_specs=ANY,
+        in_specs=[ANY],
+        out_specs=HBM,
         scratch_shapes=[pltpu.SemaphoreType.DMA],
         compiler_params=SMALL,
         name="place",
@@ -204,8 +216,8 @@
     fwd_out = pl.pallas_call(
         functools.partial(place_kernel, True),
         out_shape=struct(residual.shape),
-        in_specs=[VMEM, ANY],
-        out_specs=ANY,
+        in_specs=[ANY, HBM],
+        out_specs=HBM,
         input_output_aliases={1: 0},
         scratch_shapes=[pltpu.SemaphoreType.DMA],
         compiler_params=SMALL,

time: 83.9 us -> 83.6 us (level)
  waiting for transfers between devices: 27.7 us -> 25.7 us
  local copies, waits for them, and re-layouts: 0.05 us -> 1.8 us
  other arithmetic: 3.03 us -> 1.8 us
  Pallas kernels: 10.6 us -> 11.7 us
    ppermute x2, waiting for transfers between devices: 19.6 us -> 16.2 us  [shifted(): lax.ppermute(block, axis, [((i - distance) % count, i) for i in range(cou...]
    pallas_call x1 -> x2, Pallas kernels: 4.1 us -> 5.88 us  [the longest x1 3.39 us: step(): pl.pallas_call(grad_kernel, out_shape=struct((rows, out_proj.shape[1])),...]
    unnamed x4 -> x6, local copies, waits for them, and re-layouts: 0.01 us -> 1.77 us
    all_to_all x1, waiting for transfers between devices: 6.34 us -> 7.96 us  [exchanged(): lax.all_to_all(blocks, 'tensor', 0, 0, axis_index_groups=groups, tiled=True)]
    reshape x1, other arithmetic: 2.11 us -> 0.88 us  [step(): partial = partial.reshape(chips, share, width)]
  transfers between devices with their start and end apart: 5 -> 5, of which waited for: 4 -> 4; matrix products, arithmetic and copies ran while one was open for 0% -> 0% of each run, Pallas kernels for 8% -> 10%
where the time goes in v4:
time: 83.6 us; the launch traced here: 83.1 us
  starting transfers between devices  28.5 us (34%)
  waiting for transfers between devices  25.7 us (31%)
  blocking collectives  12.8 us (15%)
  Pallas kernels  11.7 us (14%)
  local copies, waits for them, and re-layouts  1.8 us (2%)
  other arithmetic  1.8 us (2%)
    ppermute x2, starting transfers between devices, crossed(): lax.ppermute(block, 'tensor', [(i, i ^ 1) for i in range(lax.axis_size('t...  21.2 us
    ppermute x2, waiting for transfers between devices, shifted(): lax.ppermute(block, axis, [((i - distance) % count, i) for i in range(cou...  16.2 us
    all_to_all x1, blocking collectives, exchanged(): lax.all_to_all(blocks, 'tensor', 0, 0, axis_index_groups=groups, tiled=True)  12.8 us
    all_to_all x1, waiting for transfers between devices, exchanged(): lax.all_to_all(blocks, 'tensor', 0, 0, axis_index_groups=groups, tiled=True)  7.96 us
    ppermute x2, starting transfers between devices, shifted(): lax.ppermute(block, axis, [((i - distance) % count, i) for i in range(cou...  3.84 us
    all_to_all x1, starting transfers between devices, exchanged(): lax.all_to_all(blocks, 'tensor', 0, 0, axis_index_groups=groups, tiled=True)  3.49 us
    pallas_call x1, Pallas kernels, step(): pl.pallas_call(grad_kernel, out_shape=struct((rows, out_proj.shape[1])),...  3.39 us
    pallas_call x1, Pallas kernels, step(): pl.pallas_call(pick_kernel, out_shape=(struct((2, *attn_in.shape[1:])), s...  2.49 us
  transfers between devices with their start and end apart: 5, of which 4 were waited for; matrix products, arithmetic and copies ran while one was open for 0% of the time, Pallas kernels for 10%

profile of v4, /device:TPU:1, one launch (start us, length us, event | category | flops | bytes accessed | tf_op | source)
XLA Modules:
  0.0 83.1 jit_solution(5330497100143630541)
XLA Ops:
  0.6 0.0 copy-start
  0.6 0.9 %copy-done = bf16[1,3,128,256]{3,2,1,0:T(8,128)(2,1)S(1)} copy-done((bf16[1,3,128,256]{3,2,1,0:T(8,128)(2,1)S(1)}, bf16[1,3,128,256]{3,2,1,0:T(8,128)(2,1)}, u32[]{:S(2)}) %copy-start) | copy-done | bytes 196632
  1.6 2.5 %front.1 = (f32[64,4096]{1,0:T(8,128)S(1)}, bf16[64,4096]{1,0:T(8,128)(2,1)S(1)}) custom-call(bf16[1,3,128,256]{3,2,1,0:T(8,128)(2,1)S(1)} %copy-done, bf16[1,256,4096]{2,1,0:T(8,128)(2,1)} %weight_hbm.3), custom_call_target="tpu_custom_call" | custom-call | tf_op jit(solution)/shard_map/front/pallas_call | solution.py:151
  4.0 16.0 %collective-permute-start = (bf16[64,4096]{1,0:T(8,128)(2,1)S(1)}, bf16[64,4096]{1,0:T(8,128)(2,1)S(1)}, u32[]{:S(2)}, u32[]{:S(2)}) collective-permute-start(bf16[64,4096]{1,0:T(8,128)(2,1)S(1)} %get-tuple-element.11), channel_id=1, source_target_pairs={{0,1},{1,0},{2,3},{3,2},{4,5},{5,4},{6,7},{7,6},{8,9},{9,8},{10,11... | collective-permute-start | bytes 1572872 | tf_op jit(solution)/shard_map/ppermute | solution.py:138
  20.1 1.5 %collective-permute-done = bf16[64,4096]{1,0:T(8,128)(2,1)S(1)} collective-permute-done((bf16[64,4096]{1,0:T(8,128)(2,1)S(1)}, bf16[64,4096]{1,0:T(8,128)(2,1)S(1)}, u32[]{:S(2)}, u32[]{:S(2)}) %collective-permute-start) | collective-permute-done | bytes 524320 | tf_op jit(solution)/shard_map/ppermute | solution.py:138
  21.6 0.9 %fusion = bf16[8,8,4096]{2,1,0:T(8,128)(2,1)} fusion(f32[64,4096]{1,0:T(8,128)S(1)} %get-tuple-element.10, bf16[64,4096]{1,0:T(8,128)(2,1)S(1)} %collective-permute-done), kind=kLoop, calls=%fused_computation.1 | loop fusion | flops 786432 | bytes 2097152 | tf_op jit(solution)/shard_map/reshape | solution.py:168
  22.5 3.5 %all-to-all-start = ((bf16[8,8,4096]{2,1,0:T(8,128)(2,1)}), bf16[8,8,4096]{2,1,0:T(8,128)(2,1)S(1)}, u32[]{:S(2)}, u32[]{:S(2)}) async-start(bf16[8,8,4096]{2,1,0:T(8,128)(2,1)} %fusion), calls=%async_computation | async-start | bytes 1048576 | tf_op jit(solution)/shard_map/all_to_all | solution.py:144
  26.0 2.5 %pick.1 = (bf16[2,3,128,256]{3,2,1,0:T(8,128)(2,1)}, bf16[8,4096]{1,0:T(8,128)(2,1)}) custom-call(s32[64]{0:T(128)} %slots.1, bf16[1,2,3,128,256]{4,3,2,1,0:T(8,128)(2,1)} %stash.1, bf16[1,3,128,256]{3,2,1,0:T(8,128)(2,1)} %qkv_hbm.1, bf16[1,128,4096]{2,1,0:T(8,128)(2,1)} %residual.1), custom_call_target="tpu_custom_call" | custom-call | tf_op jit(solution)/shard_map/pick/pallas_call | solution.py:170
  28.5 0.0 copy-start.2
  28.5 8.0 %all-to-all-done = bf16[8,8,4096]{2,1,0:T(8,128)(2,1)S(1)} async-done(((bf16[8,8,4096]{2,1,0:T(8,128)(2,1)}), bf16[8,8,4096]{2,1,0:T(8,128)(2,1)S(1)}, u32[]{:S(2)}, u32[]{:S(2)}) %all-to-all-start) | async-done | bytes 524320 | tf_op jit(solution)/shard_map/all_to_all | solution.py:144
  36.4 0.9 %fusion.1 = bf16[8,4096]{1,0:T(8,128)(2,1)S(1)} fusion(bf16[8,4096]{1,0:T(8,128)(2,1)} %get-tuple-element.9, bf16[8,8,4096]{2,1,0:T(8,128)(2,1)S(1)} %all-to-all-done), kind=kLoop, calls=%fused_computation.3 | loop fusion | flops 589824 | bytes 655360 | tf_op jit(solution)/shard_map/convert_element_type | solution.py:194
  37.3 1.9 %collective-permute-start.1 = (bf16[8,4096]{1,0:T(8,128)(2,1)S(1)}, bf16[8,4096]{1,0:T(8,128)(2,1)S(1)}, u32[]{:S(2)}, u32[]{:S(2)}) collective-permute-start(bf16[8,4096]{1,0:T(8,128)(2,1)S(1)} %fusion.1), channel_id=1, source_target_pairs={{1008,0},{0,16},{16,32},{32,48},{48,64},{64,80},{80,96},{96,112},{... | collective-permute-start | bytes 196616 | tf_op jit(solution)/shard_map/ppermute | solution.py:134
  39.3 9.0 %collective-permute-done.1 = bf16[8,4096]{1,0:T(8,128)(2,1)S(1)} collective-permute-done((bf16[8,4096]{1,0:T(8,128)(2,1)S(1)}, bf16[8,4096]{1,0:T(8,128)(2,1)S(1)}, u32[]{:S(2)}, u32[]{:S(2)}) %collective-permute-start.1) | collective-permute-done | bytes 65568 | tf_op jit(solution)/shard_map/ppermute | solution.py:134
  48.3 12.8 %all_to_all.10 = bf16[8,8,4096]{2,1,0:T(8,128)(2,1)S(1)} all-to-all(bf16[8,8,4096]{2,1,0:T(8,128)(2,1)S(1)} %broadcast_in_dim.2), channel_id=1, replica_groups={{0,2,4,6,8,10,12,14},{1,3,5,7,9,11,13,15},{16,18,20,22,24,26,28,30},{17..., dimensions={0} | all-to-all | bytes 1048576 | tf_op jit(solution)/shard_map/all_to_all | solution.py:144
  61.2 5.2 %collective-permute-start.2 = (bf16[64,4096]{1,0:T(8,128)(2,1)S(1)}, bf16[64,4096]{1,0:T(8,128)(2,1)S(1)}, u32[]{:S(2)}, u32[]{:S(2)}) collective-permute-start(bf16[64,4096]{1,0:T(8,128)(2,1)S(1)} %bitcast.43), channel_id=1, source_target_pairs={{0,1},{1,0},{2,3},{3,2},{4,5},{5,4},{6,7},{7,6},{8,9},{9,8},{10,11... | collective-permute-start | bytes 1572872 | tf_op jit(solution)/shard_map/ppermute | solution.py:138
  66.3 0.0 copy-done.2
  66.3 1.9 %collective-permute-start.3 = (bf16[2,3,128,256]{3,2,1,0:T(8,128)(2,1)S(1)}, bf16[2,3,128,256]{3,2,1,0:T(8,128)(2,1)S(1)}, u32[]{:S(2)}, u32[]{:S(2)}) collective-permute-start(bf16[2,3,128,256]{3,2,1,0:T(8,128)(2,1)S(1)} %copy-done.2), channel_id=1, source_target_pairs={{512,0},{528,16},{544,32},{560,48},{576,64},{592,80},{608,96},{624... | collective-permute-start | bytes 1179656 | tf_op jit(solution)/shard_map/ppermute | solution.py:134
  68.3 3.4 %gctx.1.grad_context = bf16[128,256]{1,0:T(8,128)(2,1)} custom-call(bf16[1,128,4096]{2,1,0:T(8,128)(2,1)} %grad_hbm.1, bf16[1,256,4096]{2,1,0:T(8,128)(2,1)} %weight_hbm.3), custom_call_target="tpu_custom_call" | custom-call | tf_op jit(solution)/shard_map/gctx/pallas_call | solution.py:179
  71.7 7.2 %collective-permute-done.3.pair = bf16[2,3,128,256]{3,2,1,0:T(8,128)(2,1)S(1)} collective-permute-done((bf16[2,3,128,256]{3,2,1,0:T(8,128)(2,1)S(1)}, bf16[2,3,128,256]{3,2,1,0:T(8,128)(2,1)S(1)}, u32[]{:S(2)}, u32[]{:S(2)}) %collective-permute-start.3) | collective-permute-done | bytes 393248 | tf_op jit(solution)/shard_map/ppermute | solution.py:134
  78.9 0.0 copy-start.1
  78.9 0.8 %copy-done.1 = bf16[128,256]{1,0:T(8,128)(2,1)S(1)} copy-done((bf16[128,256]{1,0:T(8,128)(2,1)S(1)}, bf16[128,256]{1,0:T(8,128)(2,1)}, u32[]{:S(2)}) %copy-start.1) | copy-done | bytes 65560
  79.7 1.7 %back.1 = (bf16[1,3,128,256]{3,2,1,0:T(8,128)(2,1)}, bf16[1,3,128,256]{3,2,1,0:T(8,128)(2,1)}) custom-call(bf16[2,3,128,256]{3,2,1,0:T(8,128)(2,1)S(1)} %collective-permute-done.3.pair, bf16[128,256]{1,0:T(8,128)(2,1)S(1)} %copy-done.1), custom_call_target="tpu_custom_call" | custom-call | tf_op jit(solution)/shard_map/back/pallas_call | solution.py:198
  81.4 0.8 place.1.refs_0_
  82.2 0.0 collective-permute-done.2.block
  82.3 0.8 join.1
  (1 shorter events, 0.0 us)
Async XLA Ops:
  0.6 0.9 %copy-start = (bf16[1,3,128,256]{3,2,1,0:T(8,128)(2,1)S(1)}, bf16[1,3,128,256]{3,2,1,0:T(8,128)(2,1)}, u32[]{:S(2)}) copy-start(bf16[1,3,128,256]{3,2,1,0:T(8,128)(2,1)} %qkv_hbm.1) | copy-start | bytes 589828
  4.0 17.5 %collective-permute-start = (bf16[64,4096]{1,0:T(8,128)(2,1)S(1)}, bf16[64,4096]{1,0:T(8,128)(2,1)S(1)}, u32[]{:S(2)}, u32[]{:S(2)}) collective-permute-start(bf16[64,4096]{1,0:T(8,128)(2,1)S(1)} %get-tuple-element.11), channel_id=1, source_target_pairs={{0,1},{1,0},{2,3},{3,2},{4,5},{5,4},{6,7},{7,6},{8,9},{9,8},{10,11... | collective-permute-start | bytes 1572872 | tf_op jit(solution)/shard_map/ppermute | solution.py:138
  22.5 14.0 %all-to-all-start = ((bf16[8,8,4096]{2,1,0:T(8,128)(2,1)}), bf16[8,8,4096]{2,1,0:T(8,128)(2,1)S(1)}, u32[]{:S(2)}, u32[]{:S(2)}) async-start(bf16[8,8,4096]{2,1,0:T(8,128)(2,1)} %fusion), calls=%async_computation | async-start | bytes 1048576 | tf_op jit(solution)/shard_map/all_to_all | solution.py:144
  28.5 37.9 %copy-start.2 = (bf16[2,3,128,256]{3,2,1,0:T(8,128)(2,1)S(1)}, bf16[2,3,128,256]{3,2,1,0:T(8,128)(2,1)}, u32[]{:S(2)}) copy-start(bf16[2,3,128,256]{3,2,1,0:T(8,128)(2,1)} %get-tuple-element.12) | copy-start | bytes 1179652
  37.3 10.9 %collective-permute-start.1 = (bf16[8,4096]{1,0:T(8,128)(2,1)S(1)}, bf16[8,4096]{1,0:T(8,128)(2,1)S(1)}, u32[]{:S(2)}, u32[]{:S(2)}) collective-permute-start(bf16[8,4096]{1,0:T(8,128)(2,1)S(1)} %fusion.1), channel_id=1, source_target_pairs={{1008,0},{0,16},{16,32},{32,48},{48,64},{64,80},{80,96},{96,112},{... | collective-permute-start | bytes 196616 | tf_op jit(solution)/shard_map/ppermute | solution.py:134
  61.2 21.1 %collective-permute-start.2 = (bf16[64,4096]{1,0:T(8,128)(2,1)S(1)}, bf16[64,4096]{1,0:T(8,128)(2,1)S(1)}, u32[]{:S(2)}, u32[]{:S(2)}) collective-permute-start(bf16[64,4096]{1,0:T(8,128)(2,1)S(1)} %bitcast.43), channel_id=1, source_target_pairs={{0,1},{1,0},{2,3},{3,2},{4,5},{5,4},{6,7},{7,6},{8,9},{9,8},{10,11... | collective-permute-start | bytes 1572872 | tf_op jit(solution)/shard_map/ppermute | solution.py:138
  66.3 12.6 %collective-permute-start.3 = (bf16[2,3,128,256]{3,2,1,0:T(8,128)(2,1)S(1)}, bf16[2,3,128,256]{3,2,1,0:T(8,128)(2,1)S(1)}, u32[]{:S(2)}, u32[]{:S(2)}) collective-permute-start(bf16[2,3,128,256]{3,2,1,0:T(8,128)(2,1)S(1)} %copy-done.2), channel_id=1, source_target_pairs={{512,0},{528,16},{544,32},{560,48},{576,64},{592,80},{608,96},{624... | collective-permute-start | bytes 1179656 | tf_op jit(solution)/shard_map/ppermute | solution.py:134
  78.9 0.8 %copy-start.1 = (bf16[128,256]{1,0:T(8,128)(2,1)S(1)}, bf16[128,256]{1,0:T(8,128)(2,1)}, u32[]{:S(2)}) copy-start(bf16[128,256]{1,0:T(8,128)(2,1)} %gctx.1.grad_context) | copy-start | bytes 196612

commit v5 on v4

--- a/solution.py
+++ b/solution.py
@@ -74,17 +74,12 @@
         store.wait()
 
 
-def pick_kernel(slots, stash, qkv, residual, pair, rows, sems):
+def pick_kernel(slots, stash, qkv, pair, sems):
     sections = lax.axis_size("pipe")
     partner = lax.rem(lax.axis_index("pipe") + sections // 2, sections)
-    share = rows.shape[0]
-    half = residual.shape[1] // 2
-    first = core_of_chip() * half + lax.div(lax.axis_index("tensor"), 2) * share
-    first = pl.multiple_of(first, share)
     copies = (
         pltpu.make_async_copy(stash.at[0, slots[partner]], pair.at[0], sems.at[0]),
         pltpu.make_async_copy(qkv.at[0], pair.at[1], sems.at[1]),
-        pltpu.make_async_copy(residual.at[0, pl.ds(first, share)], rows, sems.at[2]),
     )
     for copy in copies:
         copy.start()
@@ -105,13 +100,22 @@
 
 
 def place_kernel(other, block, *refs):
-    out, sem = refs[-2:]
+    out, sems = refs[-2:]
     half = block.shape[0]
     core = core_of_chip()
-    first = pl.multiple_of((1 - core if other else core) * half, half)
-    copy = pltpu.make_async_copy(block, out.at[0, pl.ds(first, half)], sem)
-    copy.start()
-    copy.wait()
+    first = (1 - core if other else core) * half
+    pieces = sems.shape[0]
+    share = half // pieces
+    copies = []
+    for k in range(pieces):
+        to = pl.ds(pl.multiple_of(first + k * share, share), share)
+        copies.append(
+            pltpu.make_async_copy(block.at[pl.ds(k * share, share)], out.at[0, to], sems.at[k])
+        )
+    for copy in copies:
+        copy.start()
+    for copy in copies:
+        copy.wait()
 
 
 def backward_kernel(pair, grad_context, grads, evicted):
@@ -167,14 +171,17 @@
     partial = (own + received.astype(F32)).astype(BF)
     partial = partial.reshape(chips, share, width)
     parts = exchanged(partial)
-    pair, own_rows = pl.pallas_call(
+    pair = pl.pallas_call(
         pick_kernel,
-        out_shape=(struct((2, *attn_in.shape[1:])), struct((share, width))),
-        in_specs=[SMEM, HBM, HBM, HBM],
-        out_specs=(VMEM, VMEM),
-        scratch_shapes=[pltpu.SemaphoreType.DMA((3,))],
+        out_shape=struct((2, *attn_in.shape[1:])),
+        in_specs=[SMEM, HBM, HBM],
+        out_specs=VMEM,
+        scratch_shapes=[pltpu.SemaphoreType.DMA((2,))],
         name="pick",
-    )(stash_slot, stash_slots, attn_in, residual)
+    )(stash_slot, stash_slots, attn_in)
+    first = core_of_chip() * half + lax.div(lax.axis_index("tensor"), 2) * share
+    own_rows = lax.dynamic_slice_in_dim(residual[0], first, share, 0).astype(F32)
+    own_rows = lax.optimization_barrier(own_rows)
     swapped = shifted(pair, "pipe", sections // 2)
     grad_context = pl.pallas_call(
         grad_kernel,
@@ -186,9 +193,10 @@
             pltpu.VMEM(out_proj.shape[1:], BF),
             pltpu.SemaphoreType.DMA((2,)),
         ],
+        compiler_params=pltpu.CompilerParams(vmem_limit_bytes=52 << 20),
         name="gctx",
     )(grad_in, out_proj)
-    total = own_rows.astype(F32)
+    total = own_rows
     for chip in range(chips):
         total = total + parts[chip].astype(F32)
     total = total.astype(BF)
@@ -209,7 +217,7 @@
         out_shape=struct(residual.shape),
         in_specs=[ANY],
         out_specs=HBM,
-        scratch_shapes=[pltpu.SemaphoreType.DMA],
+        scratch_shapes=[pltpu.SemaphoreType.DMA((4,))],
         compiler_params=SMALL,
         name="place",
     )(arrived)
@@ -219,7 +227,7 @@
         in_specs=[ANY, HBM],
         out_specs=HBM,
         input_output_aliases={1: 0},
-        scratch_shapes=[pltpu.SemaphoreType.DMA],
+        scratch_shapes=[pltpu.SemaphoreType.DMA((4,))],
         compiler_params=SMALL,
         name="join",
     )(other, placed)

time: 83.6 us -> 84.7 us (1.013)
  waiting for transfers between devices: 25.7 us -> 28.5 us
  Pallas kernels: 11.7 us -> 10.8 us
    all_to_all x1, waiting for transfers between devices: 7.96 us -> 9.6 us  [exchanged(): lax.all_to_all(blocks, 'tensor', 0, 0, axis_index_groups=groups, tiled=True)]
    ppermute x2, waiting for transfers between devices: 16.2 us -> 17.3 us  [shifted(): lax.ppermute(block, axis, [((i - distance) % count, i) for i in range(cou...]
    pallas_call x1, Pallas kernels: 3.39 us -> 2.5 us  [step(): pl.pallas_call(grad_kernel, out_shape=struct((rows, out_proj.shape[1])),...]
    convert_element_type x0 -> x1, other arithmetic: none -> 0.85 us  [step(): lax.dynamic_slice_in_dim(residual[0], first, share, 0).astype(F32)]
    unnamed x6 -> x4, local copies, waits for them, and re-layouts: 1.77 us -> 0.93 us
  transfers between devices with their start and end apart: 5 -> 5, of which waited for: 4 -> 4; matrix products, arithmetic and copies ran while one was open for 0% -> 1% of each run, Pallas kernels for 10% -> 9%
where the time goes in v5:
time: 84.7 us; the launch traced here: 84.2 us
  starting transfers between devices  28.7 us (34%)
  waiting for transfers between devices  28.5 us (34%)
  blocking collectives  12.8 us (15%)
  Pallas kernels  10.8 us (13%)
  other arithmetic  1.81 us (2%)
  local copies, waits for them, and re-layouts  0.96 us (1%)
    ppermute x2, starting transfers between devices, crossed(): lax.ppermute(block, 'tensor', [(i, i ^ 1) for i in range(lax.axis_size('t...  21.2 us
    ppermute x2, waiting for transfers between devices, shifted(): lax.ppermute(block, axis, [((i - distance) % count, i) for i in range(cou...  17.3 us
    all_to_all x1, blocking collectives, exchanged(): lax.all_to_all(blocks, 'tensor', 0, 0, axis_index_groups=groups, tiled=True)  12.8 us
    all_to_all x1, waiting for transfers between devices, exchanged(): lax.all_to_all(blocks, 'tensor', 0, 0, axis_index_groups=groups, tiled=True)  9.6 us
    ppermute x2, starting transfers between devices, shifted(): lax.ppermute(block, axis, [((i - distance) % count, i) for i in range(cou...  3.84 us
    all_to_all x1, starting transfers between devices, exchanged(): lax.all_to_all(blocks, 'tensor', 0, 0, axis_index_groups=groups, tiled=True)  3.63 us
    pallas_call x1, Pallas kernels, step(): pl.pallas_call(grad_kernel, out_shape=struct((rows, out_proj.shape[1])),...  2.5 us
    pallas_call x1, Pallas kernels, step(): pl.pallas_call(pick_kernel, out_shape=struct((2, *attn_in.shape[1:])), in...  2.46 us
  transfers between devices with their start and end apart: 5, of which 4 were waited for; matrix products, arithmetic and copies ran while one was open for 1% of the time, Pallas kernels for 9%

profile of v5, /device:TPU:1, one launch (start us, length us, event | category | flops | bytes accessed | tf_op | source)
XLA Modules:
  0.0 84.2 jit_solution(14644396595294755377)
XLA Ops:
  0.6 0.0 copy-start.1
  0.6 0.9 %copy-done.1 = bf16[1,3,128,256]{3,2,1,0:T(8,128)(2,1)S(1)} copy-done((bf16[1,3,128,256]{3,2,1,0:T(8,128)(2,1)S(1)}, bf16[1,3,128,256]{3,2,1,0:T(8,128)(2,1)}, u32[]{:S(2)}) %copy-start.1) | copy-done | bytes 196632
  1.6 2.5 %front.1 = (f32[64,4096]{1,0:T(8,128)S(1)}, bf16[64,4096]{1,0:T(8,128)(2,1)S(1)}) custom-call(bf16[1,3,128,256]{3,2,1,0:T(8,128)(2,1)S(1)} %copy-done.1, bf16[1,256,4096]{2,1,0:T(8,128)(2,1)} %weight_hbm.3), custom_call_target="tpu_custom_call" | custom-call | tf_op jit(solution)/shard_map/front/pallas_call | solution.py:155
  4.0 16.0 %collective-permute-start = (bf16[64,4096]{1,0:T(8,128)(2,1)S(1)}, bf16[64,4096]{1,0:T(8,128)(2,1)S(1)}, u32[]{:S(2)}, u32[]{:S(2)}) collective-permute-start(bf16[64,4096]{1,0:T(8,128)(2,1)S(1)} %get-tuple-element.8), channel_id=1, source_target_pairs={{0,1},{1,0},{2,3},{3,2},{4,5},{5,4},{6,7},{7,6},{8,9},{9,8},{10,11... | collective-permute-start | bytes 1572872 | tf_op jit(solution)/shard_map/ppermute | solution.py:142
  20.1 1.5 %collective-permute-done = bf16[64,4096]{1,0:T(8,128)(2,1)S(1)} collective-permute-done((bf16[64,4096]{1,0:T(8,128)(2,1)S(1)}, bf16[64,4096]{1,0:T(8,128)(2,1)S(1)}, u32[]{:S(2)}, u32[]{:S(2)}) %collective-permute-start) | collective-permute-done | bytes 524320 | tf_op jit(solution)/shard_map/ppermute | solution.py:142
  21.6 0.9 %fusion = bf16[8,8,4096]{2,1,0:T(8,128)(2,1)} fusion(f32[64,4096]{1,0:T(8,128)S(1)} %get-tuple-element.7, bf16[64,4096]{1,0:T(8,128)(2,1)S(1)} %collective-permute-done), kind=kLoop, calls=%fused_computation.1 | loop fusion | flops 786432 | bytes 2097152 | tf_op jit(solution)/shard_map/reshape | solution.py:172
  22.5 0.0 copy-start
  22.5 3.6 %all-to-all-start = ((bf16[8,8,4096]{2,1,0:T(8,128)(2,1)}), bf16[8,8,4096]{2,1,0:T(8,128)(2,1)S(1)}, u32[]{:S(2)}, u32[]{:S(2)}) async-start(bf16[8,8,4096]{2,1,0:T(8,128)(2,1)} %fusion), calls=%async_computation | async-start | bytes 1048576 | tf_op jit(solution)/shard_map/all_to_all | solution.py:148
  26.1 0.9 %bitcast_convert_fusion = f32[8,4096]{1,0:T(8,128)S(1)} fusion(bf16[1,128,4096]{2,1,0:T(8,128)(2,1)} %param.6, s32[]{:T(128)S(6)} %select_n.3), kind=kLoop, calls=%fused_computation.19 | loop fusion | flops 32768 | bytes 196612 | tf_op jit(solution)/shard_map/convert_element_type | solution.py:183
  27.0 9.6 %all-to-all-done = bf16[8,8,4096]{2,1,0:T(8,128)(2,1)S(1)} async-done(((bf16[8,8,4096]{2,1,0:T(8,128)(2,1)}), bf16[8,8,4096]{2,1,0:T(8,128)(2,1)S(1)}, u32[]{:S(2)}, u32[]{:S(2)}) %all-to-all-start) | async-done | bytes 524320 | tf_op jit(solution)/shard_map/all_to_all | solution.py:148
  36.6 0.1 fusion.1
  36.6 1.9 %collective-permute-start.1 = (bf16[8,4096]{1,0:T(8,128)(2,1)S(1)}, bf16[8,4096]{1,0:T(8,128)(2,1)S(1)}, u32[]{:S(2)}, u32[]{:S(2)}) collective-permute-start(bf16[8,4096]{1,0:T(8,128)(2,1)S(1)} %fusion.1), channel_id=1, source_target_pairs={{1008,0},{0,16},{16,32},{32,48},{48,64},{64,80},{80,96},{96,112},{... | collective-permute-start | bytes 196616 | tf_op jit(solution)/shard_map/ppermute | solution.py:138
  38.6 9.0 %collective-permute-done.1 = bf16[8,4096]{1,0:T(8,128)(2,1)S(1)} collective-permute-done((bf16[8,4096]{1,0:T(8,128)(2,1)S(1)}, bf16[8,4096]{1,0:T(8,128)(2,1)S(1)}, u32[]{:S(2)}, u32[]{:S(2)}) %collective-permute-start.1) | collective-permute-done | bytes 65568 | tf_op jit(solution)/shard_map/ppermute | solution.py:138
  47.6 12.8 %all_to_all.10 = bf16[8,8,4096]{2,1,0:T(8,128)(2,1)S(1)} all-to-all(bf16[8,8,4096]{2,1,0:T(8,128)(2,1)S(1)} %broadcast_in_dim.2), channel_id=1, replica_groups={{0,2,4,6,8,10,12,14},{1,3,5,7,9,11,13,15},{16,18,20,22,24,26,28,30},{17..., dimensions={0} | all-to-all | bytes 1048576 | tf_op jit(solution)/shard_map/all_to_all | solution.py:148
  60.4 5.2 %collective-permute-start.2 = (bf16[64,4096]{1,0:T(8,128)(2,1)S(1)}, bf16[64,4096]{1,0:T(8,128)(2,1)S(1)}, u32[]{:S(2)}, u32[]{:S(2)}) collective-permute-start(bf16[64,4096]{1,0:T(8,128)(2,1)S(1)} %bitcast.46), channel_id=1, source_target_pairs={{0,1},{1,0},{2,3},{3,2},{4,5},{5,4},{6,7},{7,6},{8,9},{9,8},{10,11... | collective-permute-start | bytes 1572872 | tf_op jit(solution)/shard_map/ppermute | solution.py:142
  65.6 2.5 %pick.1 = bf16[2,3,128,256]{3,2,1,0:T(8,128)(2,1)} custom-call(s32[64]{0:T(128)} %slots.1, bf16[1,2,3,128,256]{4,3,2,1,0:T(8,128)(2,1)} %stash.1, bf16[1,3,128,256]{3,2,1,0:T(8,128)(2,1)} %qkv.1), custom_call_target="tpu_custom_call" | custom-call | tf_op jit(solution)/shard_map/pick/pallas_call | solution.py:174
  68.1 1.9 %collective-permute-start.3 = (bf16[2,3,128,256]{3,2,1,0:T(8,128)(2,1)}, bf16[2,3,128,256]{3,2,1,0:T(8,128)(2,1)S(1)}, u32[]{:S(2)}, u32[]{:S(2)}) collective-permute-start(bf16[2,3,128,256]{3,2,1,0:T(8,128)(2,1)} %pick.1), channel_id=1, source_target_pairs={{512,0},{528,16},{544,32},{560,48},{576,64},{592,80},{608,96},{624... | collective-permute-start | bytes 1179656 | tf_op jit(solution)/shard_map/ppermute | solution.py:138
  70.0 0.0 copy-done
  70.0 2.5 %gctx.1.grad_context = bf16[128,256]{1,0:T(8,128)(2,1)S(1)} custom-call(bf16[1,128,4096]{2,1,0:T(8,128)(2,1)S(1)} %copy-done, bf16[1,256,4096]{2,1,0:T(8,128)(2,1)} %weight_hbm.3), custom_call_target="tpu_custom_call" | custom-call | tf_op jit(solution)/shard_map/gctx/pallas_call | solution.py:186
  72.5 8.3 %collective-permute-done.3.pair = bf16[2,3,128,256]{3,2,1,0:T(8,128)(2,1)S(1)} collective-permute-done((bf16[2,3,128,256]{3,2,1,0:T(8,128)(2,1)}, bf16[2,3,128,256]{3,2,1,0:T(8,128)(2,1)S(1)}, u32[]{:S(2)}, u32[]{:S(2)}) %collective-permute-start.3) | collective-permute-done | bytes 393248 | tf_op jit(solution)/shard_map/ppermute | solution.py:138
  80.9 1.7 %back.1 = (bf16[1,3,128,256]{3,2,1,0:T(8,128)(2,1)}, bf16[1,3,128,256]{3,2,1,0:T(8,128)(2,1)}) custom-call(bf16[2,3,128,256]{3,2,1,0:T(8,128)(2,1)S(1)} %collective-permute-done.3.pair, bf16[128,256]{1,0:T(8,128)(2,1)S(1)} %gctx.1.grad_context), custom_call_target="tpu_custom_call" | custom-call | tf_op jit(solution)/shard_map/back/pallas_call | solution.py:206
  82.6 0.8 place.1.refs_0_
  83.4 0.0 collective-permute-done.2.block
  83.4 0.8 join.1
  (1 shorter events, 0.0 us)
Async XLA Ops:
  0.6 0.9 %copy-start.1 = (bf16[1,3,128,256]{3,2,1,0:T(8,128)(2,1)S(1)}, bf16[1,3,128,256]{3,2,1,0:T(8,128)(2,1)}, u32[]{:S(2)}) copy-start(bf16[1,3,128,256]{3,2,1,0:T(8,128)(2,1)} %qkv.1) | copy-start | bytes 589828
  4.0 17.5 %collective-permute-start = (bf16[64,4096]{1,0:T(8,128)(2,1)S(1)}, bf16[64,4096]{1,0:T(8,128)(2,1)S(1)}, u32[]{:S(2)}, u32[]{:S(2)}) collective-permute-start(bf16[64,4096]{1,0:T(8,128)(2,1)S(1)} %get-tuple-element.8), channel_id=1, source_target_pairs={{0,1},{1,0},{2,3},{3,2},{4,5},{5,4},{6,7},{7,6},{8,9},{9,8},{10,11... | collective-permute-start | bytes 1572872 | tf_op jit(solution)/shard_map/ppermute | solution.py:142
  22.5 47.6 %copy-start = (bf16[1,128,4096]{2,1,0:T(8,128)(2,1)S(1)}, bf16[1,128,4096]{2,1,0:T(8,128)(2,1)}, u32[]{:S(2)}) copy-start(bf16[1,128,4096]{2,1,0:T(8,128)(2,1)} %grad_hbm.1) | copy-start | bytes 3145732
  22.5 14.1 %all-to-all-start = ((bf16[8,8,4096]{2,1,0:T(8,128)(2,1)}), bf16[8,8,4096]{2,1,0:T(8,128)(2,1)S(1)}, u32[]{:S(2)}, u32[]{:S(2)}) async-start(bf16[8,8,4096]{2,1,0:T(8,128)(2,1)} %fusion), calls=%async_computation | async-start | bytes 1048576 | tf_op jit(solution)/shard_map/all_to_all | solution.py:148
  36.6 10.9 %collective-permute-start.1 = (bf16[8,4096]{1,0:T(8,128)(2,1)S(1)}, bf16[8,4096]{1,0:T(8,128)(2,1)S(1)}, u32[]{:S(2)}, u32[]{:S(2)}) collective-permute-start(bf16[8,4096]{1,0:T(8,128)(2,1)S(1)} %fusion.1), channel_id=1, source_target_pairs={{1008,0},{0,16},{16,32},{32,48},{48,64},{64,80},{80,96},{96,112},{... | collective-permute-start | bytes 196616 | tf_op jit(solution)/shard_map/ppermute | solution.py:138
  60.4 23.0 %collective-permute-start.2 = (bf16[64,4096]{1,0:T(8,128)(2,1)S(1)}, bf16[64,4096]{1,0:T(8,128)(2,1)S(1)}, u32[]{:S(2)}, u32[]{:S(2)}) collective-permute-start(bf16[64,4096]{1,0:T(8,128)(2,1)S(1)} %bitcast.46), channel_id=1, source_target_pairs={{0,1},{1,0},{2,3},{3,2},{4,5},{5,4},{6,7},{7,6},{8,9},{9,8},{10,11... | collective-permute-start | bytes 1572872 | tf_op jit(solution)/shard_map/ppermute | solution.py:142
  68.1 12.8 %collective-permute-start.3 = (bf16[2,3,128,256]{3,2,1,0:T(8,128)(2,1)}, bf16[2,3,128,256]{3,2,1,0:T(8,128)(2,1)S(1)}, u32[]{:S(2)}, u32[]{:S(2)}) collective-permute-start(bf16[2,3,128,256]{3,2,1,0:T(8,128)(2,1)} %pick.1), channel_id=1, source_target_pairs={{512,0},{528,16},{544,32},{560,48},{576,64},{592,80},{608,96},{624... | collective-permute-start | bytes 1179656 | tf_op jit(solution)/shard_map/ppermute | solution.py:138

commit v6 on v5

--- a/solution.py
+++ b/solution.py
@@ -41,7 +41,7 @@
     return weights / jnp.sum(weights, axis=1, keepdims=True)
 
 
-def forward_kernel(qkv_hbm, weight_hbm, own, theirs_hbm, qkv, weight, context, theirs, sems):
+def forward_kernel(qkv_hbm, weight_hbm, own, theirs, qkv, weight, context, sems):
     half, width = theirs.shape
     depth = weight.shape[0] // 2
     load_qkv = pltpu.make_async_copy(qkv_hbm.at[0], qkv, sems.at[0])
@@ -63,15 +63,10 @@
     both = jnp.concatenate([context[pl.ds(first, half), :], context[pl.ds(second, half), :]], axis=0)
     for load in loads:
         load.wait()
-    stores = []
-    for n, c in enumerate((slice(0, width // 2), slice(width // 2, width))):
+    for c in (slice(0, width // 2), slice(width // 2, width)):
         product = dot(both, weight[:, c], 1, 0)
         theirs[:, c] = product[:half].astype(BF)
         own[:, c] = product[half:]
-        stores.append(pltpu.make_async_copy(theirs.at[:, c], theirs_hbm.at[:, c], sems.at[3 + n]))
-        stores[-1].start()
-    for store in stores:
-        store.wait()
 
 
 def pick_kernel(slots, stash, qkv, pair, sems):
@@ -154,17 +149,16 @@
     chips, half, share = members // 2, rows // 2, rows // members
     own, theirs = pl.pallas_call(
         forward_kernel,
-        out_shape=(struct((half, width), F32), struct((half, width))),
+        out_shape=(pltpu.VMEM((half, width), F32), pltpu.VMEM((half, width), BF)),
         in_specs=[HBM, HBM],
-        out_specs=(VMEM, HBM),
+        out_specs=(VMEM, VMEM),
         scratch_shapes=[
             pltpu.VMEM(attn_in.shape[1:], BF),
             pltpu.VMEM(out_proj.shape[1:], BF),
             pltpu.VMEM((rows, out_proj.shape[1]), BF),
-            pltpu.VMEM((half, width), BF),
-            pltpu.SemaphoreType.DMA((5,)),
+            pltpu.SemaphoreType.DMA((3,)),
         ],
-        compiler_params=pltpu.CompilerParams(vmem_limit_bytes=52 << 20),
+        compiler_params=pltpu.CompilerParams(vmem_limit_bytes=53 << 20),
         name="front",
     )(attn_in, out_proj)
     received = crossed(theirs)
@@ -173,7 +167,7 @@
     parts = exchanged(partial)
     pair = pl.pallas_call(
         pick_kernel,
-        out_shape=struct((2, *attn_in.shape[1:])),
+        out_shape=pltpu.VMEM((2, *attn_in.shape[1:]), BF),
         in_specs=[SMEM, HBM, HBM],
         out_specs=VMEM,
         scratch_shapes=[pltpu.SemaphoreType.DMA((2,))],
@@ -248,4 +242,6 @@
         P("pipe", None, None, "tensor"),
         P("pipe", None, None, "tensor"),
     )
-    return jax.shard_map(step, mesh=mesh, in_specs=in_specs, out_specs=out_specs, check_vma=False)
+    return jax.shard_map(
+        step, mesh=mesh, in_specs=in_specs, out_specs=out_specs, check_vma=False
+    )

time: 84.7 us -> 82.5 us (0.974)
  Pallas kernels: 10.8 us -> 9.77 us
  local copies, waits for them, and re-layouts: 0.96 us -> 0.04 us
    pallas_call x2, Pallas kernels: 4.92 us -> 3.9 us  [the longest x1 2.18 us: step(): pl.pallas_call(forward_kernel, out_shape=(pltpu.VMEM((half, width), F32),...]
    unnamed x4 -> x2, local copies, waits for them, and re-layouts: 0.93 us -> 0.01 us
  transfers between devices with their start and end apart: 5 -> 5, of which waited for: 4 -> 4; matrix products, arithmetic and copies ran while one was open for 1% -> 1% of each run, Pallas kernels for 9% -> 8%
where the time goes in v6:
time: 82.5 us; the launch traced here: 82.1 us
  starting transfers between devices  28.7 us (35%)
  waiting for transfers between devices  28.2 us (34%)
  blocking collectives  12.8 us (16%)
  Pallas kernels  9.77 us (12%)
  other arithmetic  1.81 us (2%)
    ppermute x2, starting transfers between devices, crossed(): lax.ppermute(block, 'tensor', [(i, i ^ 1) for i in range(lax.axis_size('t...  21.2 us
    ppermute x2, waiting for transfers between devices, shifted(): lax.ppermute(block, axis, [((i - distance) % count, i) for i in range(cou...  17.1 us
    all_to_all x1, blocking collectives, exchanged(): lax.all_to_all(blocks, 'tensor', 0, 0, axis_index_groups=groups, tiled=True)  12.8 us
    all_to_all x1, waiting for transfers between devices, exchanged(): lax.all_to_all(blocks, 'tensor', 0, 0, axis_index_groups=groups, tiled=True)  9.6 us
    ppermute x2, starting transfers between devices, shifted(): lax.ppermute(block, axis, [((i - distance) % count, i) for i in range(cou...  3.84 us
    all_to_all x1, starting transfers between devices, exchanged(): lax.all_to_all(blocks, 'tensor', 0, 0, axis_index_groups=groups, tiled=True)  3.63 us
    pallas_call x1, Pallas kernels, step(): pl.pallas_call(grad_kernel, out_shape=struct((rows, out_proj.shape[1])),...  2.5 us
    pallas_call x1, Pallas kernels, step(): pl.pallas_call(forward_kernel, out_shape=(pltpu.VMEM((half, width), F32),...  2.18 us
  transfers between devices with their start and end apart: 5, of which 4 were waited for; matrix products, arithmetic and copies ran while one was open for 1% of the time, Pallas kernels for 8%

profile of v6, /device:TPU:1, one launch (start us, length us, event | category | flops | bytes accessed | tf_op | source)
XLA Modules:
  0.0 82.1 jit_solution(10071314024934579628)
XLA Ops:
  0.6 2.2 %front.1 = (f32[64,4096]{1,0:T(8,128)S(1)}, bf16[64,4096]{1,0:T(8,128)(2,1)S(1)}) custom-call(bf16[1,3,128,256]{3,2,1,0:T(8,128)(2,1)} %qkv.1, bf16[1,256,4096]{2,1,0:T(8,128)(2,1)} %weight_hbm.3), custom_call_target="tpu_custom_call" | custom-call | tf_op jit(solution)/shard_map/front/pallas_call | solution.py:150
  2.8 16.0 %collective-permute-start = (bf16[64,4096]{1,0:T(8,128)(2,1)S(1)}, bf16[64,4096]{1,0:T(8,128)(2,1)S(1)}, u32[]{:S(2)}, u32[]{:S(2)}) collective-permute-start(bf16[64,4096]{1,0:T(8,128)(2,1)S(1)} %get-tuple-element.8), channel_id=1, source_target_pairs={{0,1},{1,0},{2,3},{3,2},{4,5},{5,4},{6,7},{7,6},{8,9},{9,8},{10,11... | collective-permute-start | bytes 1572872 | tf_op jit(solution)/shard_map/ppermute | solution.py:137
  18.8 1.5 %collective-permute-done = bf16[64,4096]{1,0:T(8,128)(2,1)S(1)} collective-permute-done((bf16[64,4096]{1,0:T(8,128)(2,1)S(1)}, bf16[64,4096]{1,0:T(8,128)(2,1)S(1)}, u32[]{:S(2)}, u32[]{:S(2)}) %collective-permute-start) | collective-permute-done | bytes 524320 | tf_op jit(solution)/shard_map/ppermute | solution.py:137
  20.4 0.9 %fusion = bf16[8,8,4096]{2,1,0:T(8,128)(2,1)} fusion(f32[64,4096]{1,0:T(8,128)S(1)} %get-tuple-element.7, bf16[64,4096]{1,0:T(8,128)(2,1)S(1)} %collective-permute-done), kind=kLoop, calls=%fused_computation.1 | loop fusion | flops 786432 | bytes 2097152 | tf_op jit(solution)/shard_map/reshape | solution.py:166
  21.2 0.0 copy-start
  21.2 3.6 %all-to-all-start = ((bf16[8,8,4096]{2,1,0:T(8,128)(2,1)}), bf16[8,8,4096]{2,1,0:T(8,128)(2,1)S(1)}, u32[]{:S(2)}, u32[]{:S(2)}) async-start(bf16[8,8,4096]{2,1,0:T(8,128)(2,1)} %fusion), calls=%async_computation | async-start | bytes 1048576 | tf_op jit(solution)/shard_map/all_to_all | solution.py:143
  24.9 0.9 %bitcast_convert_fusion = f32[8,4096]{1,0:T(8,128)S(1)} fusion(bf16[1,128,4096]{2,1,0:T(8,128)(2,1)} %param.6, s32[]{:T(128)S(6)} %select_n.3), kind=kLoop, calls=%fused_computation.19 | loop fusion | flops 32768 | bytes 196612 | tf_op jit(solution)/shard_map/convert_element_type | solution.py:177
  25.7 9.6 %all-to-all-done = bf16[8,8,4096]{2,1,0:T(8,128)(2,1)S(1)} async-done(((bf16[8,8,4096]{2,1,0:T(8,128)(2,1)}), bf16[8,8,4096]{2,1,0:T(8,128)(2,1)S(1)}, u32[]{:S(2)}, u32[]{:S(2)}) %all-to-all-start) | async-done | bytes 524320 | tf_op jit(solution)/shard_map/all_to_all | solution.py:143
  35.4 0.1 fusion.1
  35.4 1.9 %collective-permute-start.1 = (bf16[8,4096]{1,0:T(8,128)(2,1)S(1)}, bf16[8,4096]{1,0:T(8,128)(2,1)S(1)}, u32[]{:S(2)}, u32[]{:S(2)}) collective-permute-start(bf16[8,4096]{1,0:T(8,128)(2,1)S(1)} %fusion.1), channel_id=1, source_target_pairs={{1008,0},{0,16},{16,32},{32,48},{48,64},{64,80},{80,96},{96,112},{... | collective-permute-start | bytes 196616 | tf_op jit(solution)/shard_map/ppermute | solution.py:133
  37.4 9.0 %collective-permute-done.1 = bf16[8,4096]{1,0:T(8,128)(2,1)S(1)} collective-permute-done((bf16[8,4096]{1,0:T(8,128)(2,1)S(1)}, bf16[8,4096]{1,0:T(8,128)(2,1)S(1)}, u32[]{:S(2)}, u32[]{:S(2)}) %collective-permute-start.1) | collective-permute-done | bytes 65568 | tf_op jit(solution)/shard_map/ppermute | solution.py:133
  46.4 12.8 %all_to_all.10 = bf16[8,8,4096]{2,1,0:T(8,128)(2,1)S(1)} all-to-all(bf16[8,8,4096]{2,1,0:T(8,128)(2,1)S(1)} %broadcast_in_dim.2), channel_id=1, replica_groups={{0,2,4,6,8,10,12,14},{1,3,5,7,9,11,13,15},{16,18,20,22,24,26,28,30},{17..., dimensions={0} | all-to-all | bytes 1048576 | tf_op jit(solution)/shard_map/all_to_all | solution.py:143
  59.2 5.2 %collective-permute-start.2 = (bf16[64,4096]{1,0:T(8,128)(2,1)S(1)}, bf16[64,4096]{1,0:T(8,128)(2,1)S(1)}, u32[]{:S(2)}, u32[]{:S(2)}) collective-permute-start(bf16[64,4096]{1,0:T(8,128)(2,1)S(1)} %bitcast.46), channel_id=1, source_target_pairs={{0,1},{1,0},{2,3},{3,2},{4,5},{5,4},{6,7},{7,6},{8,9},{9,8},{10,11... | collective-permute-start | bytes 1572872 | tf_op jit(solution)/shard_map/ppermute | solution.py:137
  64.4 1.7 %pick.1 = bf16[2,3,128,256]{3,2,1,0:T(8,128)(2,1)S(1)} custom-call(s32[64]{0:T(128)} %slots.1, bf16[1,2,3,128,256]{4,3,2,1,0:T(8,128)(2,1)} %stash.1, bf16[1,3,128,256]{3,2,1,0:T(8,128)(2,1)} %qkv.1), custom_call_target="tpu_custom_call" | custom-call | tf_op jit(solution)/shard_map/pick/pallas_call | solution.py:168
  66.1 1.9 %collective-permute-start.3 = (bf16[2,3,128,256]{3,2,1,0:T(8,128)(2,1)S(1)}, bf16[2,3,128,256]{3,2,1,0:T(8,128)(2,1)S(1)}, u32[]{:S(2)}, u32[]{:S(2)}) collective-permute-start(bf16[2,3,128,256]{3,2,1,0:T(8,128)(2,1)S(1)} %pick.1), channel_id=1, source_target_pairs={{512,0},{528,16},{544,32},{560,48},{576,64},{592,80},{608,96},{624... | collective-permute-start | bytes 1179656 | tf_op jit(solution)/shard_map/ppermute | solution.py:133
  68.1 0.0 copy-done
  68.1 2.5 %gctx.1.grad_context = bf16[128,256]{1,0:T(8,128)(2,1)S(1)} custom-call(bf16[1,128,4096]{2,1,0:T(8,128)(2,1)S(1)} %copy-done, bf16[1,256,4096]{2,1,0:T(8,128)(2,1)} %weight_hbm.3), custom_call_target="tpu_custom_call" | custom-call | tf_op jit(solution)/shard_map/gctx/pallas_call | solution.py:180
  70.6 8.1 %collective-permute-done.3.pair = bf16[2,3,128,256]{3,2,1,0:T(8,128)(2,1)S(1)} collective-permute-done((bf16[2,3,128,256]{3,2,1,0:T(8,128)(2,1)S(1)}, bf16[2,3,128,256]{3,2,1,0:T(8,128)(2,1)S(1)}, u32[]{:S(2)}, u32[]{:S(2)}) %collective-permute-start.3) | collective-permute-done | bytes 393248 | tf_op jit(solution)/shard_map/ppermute | solution.py:133
  78.7 1.7 %back.1 = (bf16[1,3,128,256]{3,2,1,0:T(8,128)(2,1)}, bf16[1,3,128,256]{3,2,1,0:T(8,128)(2,1)}) custom-call(bf16[2,3,128,256]{3,2,1,0:T(8,128)(2,1)S(1)} %collective-permute-done.3.pair, bf16[128,256]{1,0:T(8,128)(2,1)S(1)} %gctx.1.grad_context), custom_call_target="tpu_custom_call" | custom-call | tf_op jit(solution)/shard_map/back/pallas_call | solution.py:200
  80.4 0.8 place.1.refs_0_
  81.2 0.0 collective-permute-done.2.block
  81.2 0.8 %join.1 = bf16[1,128,4096]{2,1,0:T(8,128)(2,1)} custom-call(bf16[64,4096]{1,0:T(8,128)(2,1)S(1)} %collective-permute-done.2.block, bf16[1,128,4096]{2,1,0:T(8,128)(2,1)} %place.1.refs_0_), custom_call_target="tpu_custom_call", output_to_operand_aliasing={{}: (1, {})} | custom-call | tf_op jit(solution)/shard_map/join/pallas_call | solution.py:218
  (1 shorter events, 0.0 us)
Async XLA Ops:
  2.8 17.5 %collective-permute-start = (bf16[64,4096]{1,0:T(8,128)(2,1)S(1)}, bf16[64,4096]{1,0:T(8,128)(2,1)S(1)}, u32[]{:S(2)}, u32[]{:S(2)}) collective-permute-start(bf16[64,4096]{1,0:T(8,128)(2,1)S(1)} %get-tuple-element.8), channel_id=1, source_target_pairs={{0,1},{1,0},{2,3},{3,2},{4,5},{5,4},{6,7},{7,6},{8,9},{9,8},{10,11... | collective-permute-start | bytes 1572872 | tf_op jit(solution)/shard_map/ppermute | solution.py:137
  21.2 46.8 %copy-start = (bf16[1,128,4096]{2,1,0:T(8,128)(2,1)S(1)}, bf16[1,128,4096]{2,1,0:T(8,128)(2,1)}, u32[]{:S(2)}) copy-start(bf16[1,128,4096]{2,1,0:T(8,128)(2,1)} %grad_hbm.1) | copy-start | bytes 3145732
  21.2 14.1 %all-to-all-start = ((bf16[8,8,4096]{2,1,0:T(8,128)(2,1)}), bf16[8,8,4096]{2,1,0:T(8,128)(2,1)S(1)}, u32[]{:S(2)}, u32[]{:S(2)}) async-start(bf16[8,8,4096]{2,1,0:T(8,128)(2,1)} %fusion), calls=%async_computation | async-start | bytes 1048576 | tf_op jit(solution)/shard_map/all_to_all | solution.py:143
  35.4 10.9 %collective-permute-start.1 = (bf16[8,4096]{1,0:T(8,128)(2,1)S(1)}, bf16[8,4096]{1,0:T(8,128)(2,1)S(1)}, u32[]{:S(2)}, u32[]{:S(2)}) collective-permute-start(bf16[8,4096]{1,0:T(8,128)(2,1)S(1)} %fusion.1), channel_id=1, source_target_pairs={{1008,0},{0,16},{16,32},{32,48},{48,64},{64,80},{80,96},{96,112},{... | collective-permute-start | bytes 196616 | tf_op jit(solution)/shard_map/ppermute | solution.py:133
  59.2 22.0 %collective-permute-start.2 = (bf16[64,4096]{1,0:T(8,128)(2,1)S(1)}, bf16[64,4096]{1,0:T(8,128)(2,1)S(1)}, u32[]{:S(2)}, u32[]{:S(2)}) collective-permute-start(bf16[64,4096]{1,0:T(8,128)(2,1)S(1)} %bitcast.46), channel_id=1, source_target_pairs={{0,1},{1,0},{2,3},{3,2},{4,5},{5,4},{6,7},{7,6},{8,9},{9,8},{10,11... | collective-permute-start | bytes 1572872 | tf_op jit(solution)/shard_map/ppermute | solution.py:137
  66.1 12.6 %collective-permute-start.3 = (bf16[2,3,128,256]{3,2,1,0:T(8,128)(2,1)S(1)}, bf16[2,3,128,256]{3,2,1,0:T(8,128)(2,1)S(1)}, u32[]{:S(2)}, u32[]{:S(2)}) collective-permute-start(bf16[2,3,128,256]{3,2,1,0:T(8,128)(2,1)S(1)} %pick.1), channel_id=1, source_target_pairs={{512,0},{528,16},{544,32},{560,48},{576,64},{592,80},{608,96},{624... | collective-permute-start | bytes 1179656 | tf_op jit(solution)/shard_map/ppermute | solution.py:133
